TPU v7x, 32 devices: a whole 2x2x4 slice. The times are simulated.
32 devices in a mesh: groups: 2 (over y), dp: 8 (over z, x), cuts: 2 (over core).
Axes of the slice: x: 2, y: 2, z: 4, core: 2. Of those that a mesh axis runs over, the one named last changes fastest.
Arguments:
- activations: bfloat16 [768, 7168], P(('groups', 'dp'), 'cuts'), parts along dimension 0, may hold values from -6 to 6
- out_grads: bfloat16 [768, 4096], P(('groups', 'dp'), 'cuts'), parts along dimension 0, may hold values from -6 to 6
- counts: int32 [16, 8], P(('groups', 'dp')), parts along dimension 0, may hold values from 1 to 24, 48 in all within a row
- doc_slots: int32 [128], P('groups'), parts along dimension 0, may hold values from 0 to 63, each once
- proj_in: bfloat16 [7168, 64], P('cuts'), may hold values from -0.0625 to 0.0625
- proj_out: bfloat16 [4096, 64], P('cuts'), may hold values from -0.09375 to 0.09375
- queries: bfloat16 [512, 4096], P(None, ('dp', 'cuts')), may hold values from -0.5 to 0.5
Outputs:
- scores: float32 [512, 128], P(('dp', 'cuts'), 'groups'), parts along dimension 1
There are 2 independent parts, one for each index of `groups`. A program takes and returns all parts, laid end to end along the dimension named above; an argument that names none is the same for every part. Nothing has to cross between parts.
Inputs may be any that keep to these rules, and one draw needn't show every extreme that they name: The 8 counts of each dp index sum to 48. `doc_slots`: each document gets a different column.
All inputs are finite; a program needn't handle non-finite values.
Results may differ from a plain program's by a relative error of at most 0.0029.
Values may be sent and summed in bfloat16 or wider, within the bound.
No kernel may reach another device: no remote copies, remote signals or barrier semaphores. Data moves between devices by JAX's collectives and lax.ppermute only.
A program may use at most 64 MiB of HBM per device.

v0:
```python
import jax
import jax.numpy as jnp
from jax import lax
from jax.sharding import PartitionSpec as P


def on_device(activations, out_grads, counts, doc_slots, proj_in, proj_out, queries):
    row_count = activations.shape[0]
    rank_size = proj_in.shape[1]
    doc_count = counts.shape[1]
    cut_count = lax.axis_size("cuts")
    data_count = lax.axis_size("dp")
    inward_part = jnp.dot(activations, proj_in, preferred_element_type=jnp.float32)
    outward_part = jnp.dot(out_grads, proj_out, preferred_element_type=jnp.float32)
    inward, outward = lax.psum((inward_part, outward_part), "cuts")
    ending = jnp.cumsum(counts[0])
    position = lax.iota(jnp.int32, row_count)
    owner_doc = jnp.sum((ending[None, :] <= position[:, None]).astype(jnp.int32), axis=1)
    member = (owner_doc[:, None] == lax.iota(jnp.int32, doc_count)[None, :]).astype(jnp.float32)
    weights = member / counts[0].astype(jnp.float32)[None, :]
    spread = (weights[:, :, None] * outward[:, None, :]).reshape(row_count, doc_count * rank_size)
    gradients = lax.dot_general(
        spread,
        inward,
        (((0,), (0,)), ((), ())),
        precision=lax.Precision.HIGHEST,
        preferred_element_type=jnp.float32,
    )
    gradients = gradients.reshape(doc_count, rank_size * rank_size).astype(jnp.bfloat16)
    slice_width = gradients.shape[1] // (cut_count * data_count)
    arranged = gradients.reshape(doc_count, data_count, cut_count, slice_width)
    picked = lax.dynamic_index_in_dim(arranged, lax.axis_index("cuts"), 2, keepdims=False).reshape(
        doc_count, data_count * slice_width
    )
    inverse = jnp.argsort(doc_slots)
    arrived = lax.all_to_all(picked, "dp", split_axis=1, concat_axis=0, tiled=True)
    ordered = jnp.take(arrived, inverse, axis=0)
    partial_value = lax.dot_general(
        queries, ordered, (((1,), (1,)), ((), ())), preferred_element_type=jnp.float32
    )
    return lax.psum_scatter(partial_value, ("dp", "cuts"), scatter_dimension=0, tiled=True)


def solution(mesh):
    placed = (
        P(("groups", "dp"), "cuts"),
        P(("groups", "dp"), "cuts"),
        P(("groups", "dp"), None),
        P("groups"),
        P("cuts", None),
        P("cuts", None),
        P(None, ("dp", "cuts")),
    )
    return jax.shard_map(
        on_device,
        mesh=mesh,
        in_specs=placed,
        out_specs=P(("dp", "cuts"), "groups"),
        check_vma=False,
    )
```

profile of v0, /device:TPU:0, one launch (start us, length us, event | category | flops | bytes accessed | tf_op | source)
XLA Modules:
  0.0 89.7 jit_solution(10809980026371094610)
XLA Ops:
  6.5 0.7 copy-done.4
  7.3 0.2 reduce-window.8
  7.4 0.1 convert_reduce_fusion
  7.5 0.1 convert_divide_fusion
  7.6 0.1 copy.20
  7.7 1.3 %fusion.5 = f32[48,64]{1,0:T(8,128)S(1)} fusion(bf16[48,3584]{1,0:T(8,128)(2,1)} %param.7, bf16[3584,64]{0,1:T(8,128)(2,1)S(1)} %copy-done), kind=kOutput, calls=%fused_computation.19 | convolution fusion | flops 22020096 | bytes 815104 | tf_op jit(solution)/shard_map/dot_general | solution.py:13
  9.0 0.0 copy-done.2
  9.0 0.2 fusion.4
  9.2 3.8 %all-reduce = (f32[48,64]{1,0:T(8,128)S(1)}, f32[48,64]{1,0:T(8,128)S(1)}) all-reduce(f32[48,64]{1,0:T(8,128)S(1)} %fusion.4, f32[48,64]{1,0:T(8,128)S(1)} %fusion.5), channel_id=1, replica_groups=mesh['groups'=2,'dp'=8,'cuts'=2] {'cuts'}, use_global_device_ids=true, to_apply=%region_3.4 | all-reduce | flops 6144 | bytes 49152 | tf_op jit(solution)/shard_map/psum | solution.py:15
  13.0 0.1 broadcast_multiply_fusion
  13.1 0.1 mul.20
  13.2 0.3 convolution_convert_fusion
  13.6 0.1 copy.21
  13.7 0.2 convert_element_type.25
  13.9 0.1 constant_dynamic-slice_fusion
  14.0 0.6 copy.28
  14.6 7.0 %all-to-all-start = ((bf16[8,8,256]{2,0,1:T(8,128)(2,1)}), bf16[8,8,256]{2,0,1:T(8,128)(2,1)S(1)}, u32[]{:S(2)}, u32[]{:S(2)}) async-start(bf16[8,8,256]{2,0,1:T(8,128)(2,1)} %bitcast.19), calls=%async_computation | async-start | bytes 65536 | tf_op jit(solution)/shard_map/all_to_all | solution.py:36
  21.6 0.0 reduce-scatter.4.cloned.1.call-start
  21.6 2.0 %sort.17 = (s32[64]{0:T(128)}, s32[64]{0:T(128)S(1)}) sort(s32[64]{0:T(128)S(1)} %copy-done.5, s32[64]{0:T(128)S(1)} %iota.15), dimensions={0}, to_apply=%region_0.0 | sort | flops 384 | bytes 1024 | tf_op jit(solution)/shard_map/jit(argsort)/sort | solution.py:35
  23.7 4.6 %all-to-all-done = bf16[8,8,256]{2,0,1:T(8,128)(2,1)S(1)} async-done(((bf16[8,8,256]{2,0,1:T(8,128)(2,1)}), bf16[8,8,256]{2,0,1:T(8,128)(2,1)S(1)}, u32[]{:S(2)}, u32[]{:S(2)}) %all-to-all-start) | async-done | bytes 32800 | tf_op jit(solution)/shard_map/all_to_all | solution.py:36
  28.3 0.7 gather_fusion
  29.0 0.2 convolution_bitcast_fusion
  29.2 0.8 copy.25
  30.0 52.9 %reduce-scatter.4.cloned.1.call-done = f32[32,64]{1,0:T(8,128)} async-done(((f32[512,64]{1,0:T(8,128)}), f32[32,64]{1,0:T(8,128)}) %reduce-scatter.4.cloned.1.call-update) | async-done | bytes 8208 | tf_op jit(solution)/shard_map/reduce_scatter | solution.py:41
  (16 shorter events, 0.1 us)
Async XLA Ops:
  6.5 1.1 %copy-start = (bf16[3584,64]{0,1:T(8,128)(2,1)S(1)}, bf16[3584,64]{0,1:T(8,128)(2,1)}, u32[]{:S(2)}) copy-start(bf16[3584,64]{0,1:T(8,128)(2,1)} %param.11) | copy-start | bytes 1376260
  6.5 0.7 copy-start.4
  7.7 1.3 %copy-start.2 = (bf16[2048,64]{0,1:T(8,128)(2,1)S(1)}, bf16[2048,64]{0,1:T(8,128)(2,1)}, u32[]{:S(2)}) copy-start(bf16[2048,64]{0,1:T(8,128)(2,1)} %param.12) | copy-start | bytes 786436
  7.7 1.3 %copy-start.3 = (bf16[48,2048]{1,0:T(8,128)(2,1)S(1)}, bf16[48,2048]{1,0:T(8,128)(2,1)}, u32[]{:S(2)}) copy-start(bf16[48,2048]{1,0:T(8,128)(2,1)} %param.8) | copy-start | bytes 589828
  13.8 7.8 %copy-start.5 = (s32[64]{0:T(128)S(1)}, s32[64]{0:T(128)}, u32[]{:S(2)}) copy-start(s32[64]{0:T(128)} %param.10) | copy-start | bytes 772
  13.9 15.0 %copy-start.1 = (bf16[512,256]{1,0:T(8,128)(2,1)S(1)}, bf16[512,256]{1,0:T(8,128)(2,1)}, u32[]{:S(2)}) copy-start(bf16[512,256]{1,0:T(8,128)(2,1)} %param.13) | copy-start | bytes 786436
  14.6 13.7 %all-to-all-start = ((bf16[8,8,256]{2,0,1:T(8,128)(2,1)}), bf16[8,8,256]{2,0,1:T(8,128)(2,1)S(1)}, u32[]{:S(2)}, u32[]{:S(2)}) async-start(bf16[8,8,256]{2,0,1:T(8,128)(2,1)} %bitcast.19), calls=%async_computation | async-start | bytes 65536 | tf_op jit(solution)/shard_map/all_to_all | solution.py:36
  21.6 61.3 %reduce-scatter.4.cloned.1.call-start = ((), (), s32[]{:S(2)}) async-start(), calls=%async_computation.2 | async-start | bytes 278528 | tf_op jit(solution)/shard_map/reduce_scatter | solution.py:41
Sparse Core Ops, SparseCore 0:
  30.1 52.6 reduce-scatter.3
where the time goes:
time: 90 us; the launch traced here: 89.7 us
  waiting for transfers between devices  57.4 us (64%)
  between operations  13.5 us (15%)
  starting transfers between devices  7.03 us (8%)
  blocking collectives  3.8 us (4%)
  local copies, waits for them, and re-layouts  3.45 us (4%)
  other arithmetic  2.51 us (3%)
  matrix products  1.98 us (2%)
    reduce_scatter x1, waiting for transfers between devices, on_device(): lax.psum_scatter(partial_value, ('dp', 'cuts'), scatter_dimension=0, tile...  52.9 us
    all_to_all x1, starting transfers between devices, on_device(): lax.all_to_all(picked, 'dp', split_axis=1, concat_axis=0, tiled=True)  6.99 us
    all_to_all x1, waiting for transfers between devices, on_device(): lax.all_to_all(picked, 'dp', split_axis=1, concat_axis=0, tiled=True)  4.56 us
    psum x1, blocking collectives, on_device(): inward, outward = lax.psum((inward_part, outward_part), 'cuts')  3.8 us
    sort x1, other arithmetic, on_device(): inverse = jnp.argsort(doc_slots)  2.03 us
  transfers between devices with their start and end apart: 2, of which 2 were waited for; matrix products, arithmetic and copies ran while one was open for 2% of the time, Pallas kernels for 0%

commit v1 on v0

v1 whole, which is shorter than its diff:
```python
import jax
import jax.numpy as jnp
from jax import lax
from jax.experimental import pallas as pl
from jax.experimental.pallas import tpu as pltpu
from jax.sharding import PartitionSpec as P

TILE = 8


def score_kernel(row_count, rank, payload_ref, query_ref, scores_ref):
    sources = payload_ref.shape[0]
    split = query_ref.shape[1] // rank
    query_rows = scores_ref.shape[0]
    chunks = query_ref.shape[0] // query_rows
    columns = scores_ref.shape[1]
    tokens = sources * row_count
    payload = payload_ref[...]
    turned = payload[:, :row_count, :].reshape(tokens, 2 * rank).T
    inward, outward = turned[:rank], turned[rank:]
    high = inward.astype(jnp.bfloat16)
    low = (inward - high.astype(jnp.float32)).astype(jnp.bfloat16)
    query = query_ref[...]
    query = jnp.concatenate([query, query], axis=1)
    blank = jnp.zeros_like(high)
    total = jnp.zeros((query_rows, tokens), jnp.float32)
    for part in range(split):
        column = [blank] * (2 * split)
        column[part], column[split + part] = high, low
        met = jnp.dot(query, jnp.concatenate(column, axis=0), preferred_element_type=jnp.float32)
        for chunk in range(chunks):
            entry = chunk * split + part
            total = total + met[chunk * query_rows:(chunk + 1) * query_rows] * outward[entry:entry + 1]
    marks = payload[:, row_count:, :].reshape(sources * TILE, 2 * rank).T
    slots = jnp.concatenate([marks[:row_count, s * TILE:s * TILE + 1] for s in range(sources)], axis=0)
    column_of = lax.broadcasted_iota(jnp.int32, (tokens, columns), 1)
    member = (slots.astype(jnp.int32) == column_of).astype(jnp.bfloat16)
    total_high = total.astype(jnp.bfloat16)
    total_low = (total - total_high.astype(jnp.float32)).astype(jnp.bfloat16)
    scores = jnp.dot(total_high, member, preferred_element_type=jnp.float32)
    scores = scores + jnp.dot(total_low, member, preferred_element_type=jnp.float32)

    @pl.when(pl.program_id(0) == 0)
    def _():
        scores_ref[...] = scores

    @pl.when(pl.program_id(0) > 0)
    def _():
        scores_ref[...] += scores


def score(payload, query, query_rows, columns, row_count, rank):
    sources = payload.shape[0]
    step = min(sources, 8)
    return pl.pallas_call(
        lambda *refs: score_kernel(row_count, rank, *refs),
        grid=(sources // step,),
        in_specs=[
            pl.BlockSpec((step,) + payload.shape[1:], lambda i: (i, 0, 0)),
            pl.BlockSpec(query.shape, lambda i: (0, 0)),
        ],
        out_specs=pl.BlockSpec((query_rows, columns), lambda i: (0, 0)),
        out_shape=jax.ShapeDtypeStruct((query_rows, columns), jnp.float32),
        compiler_params=pltpu.CompilerParams(vmem_limit_bytes=48 * 1024 * 1024),
        name="score",
    )(payload, query)


def exchange(value, axis, bit):
    count = lax.axis_size(axis)
    return lax.ppermute(value, axis, [(i, i ^ bit) for i in range(count)])


def on_device(activations, out_grads, counts, doc_slots, proj_in, proj_out, queries):
    row_count = activations.shape[0]
    rank = proj_in.shape[1]
    doc_count = counts.shape[1]
    cut_count = lax.axis_size("cuts")
    data_count = lax.axis_size("dp")
    parts = cut_count * data_count
    query_rows = queries.shape[0] // parts
    width = queries.shape[1]

    arrived = lax.all_to_all(queries, ("dp", "cuts"), split_axis=0, concat_axis=0, tiled=True)
    if width % rank:
        arrived = arrived.reshape(parts, query_rows, width).transpose(1, 0, 2)
        arrived = arrived.reshape(query_rows, -1, rank).transpose(1, 0, 2).reshape(-1, rank)

    inward = jnp.dot(activations, proj_in, preferred_element_type=jnp.float32)
    outward = jnp.dot(out_grads, proj_out, preferred_element_type=jnp.float32)
    tally = counts[0]
    order = lax.iota(jnp.int32, doc_count)
    ending = jnp.sum(jnp.where(order[None, :] <= order[:, None], tally[None, :], 0), axis=1)
    starting = ending - tally
    position = lax.iota(jnp.int32, row_count)
    member = (starting[None, :] <= position[:, None]) & (position[:, None] < ending[None, :])
    inverse = jnp.sum(jnp.where(member, 1.0 / tally.astype(jnp.float32)[None, :], 0.0), axis=1)
    own_slots = lax.dynamic_slice_in_dim(doc_slots, lax.axis_index("dp") * doc_count, doc_count)
    slots = jnp.sum(jnp.where(member, own_slots[None, :], 0), axis=1).astype(jnp.float32)
    both = jnp.concatenate([inward, outward * inverse[:, None]], axis=1)
    bit = 1
    while bit < cut_count:
        both = both + exchange(both, "cuts", bit)
        bit *= 2
    marks = jnp.zeros((TILE, 2 * rank), jnp.float32).at[0, :row_count].set(slots)
    payload = jnp.concatenate([both, marks], axis=0)[None]
    bit = 1
    while bit < data_count:
        payload = jnp.concatenate([payload, exchange(payload, "dp", bit)], axis=0)
        bit *= 2
    return score(payload, arrived, query_rows, doc_slots.shape[0], row_count, rank)


def solution(mesh):
    placed = (
        P(("groups", "dp"), "cuts"),
        P(("groups", "dp"), "cuts"),
        P(("groups", "dp"), None),
        P("groups"),
        P("cuts", None),
        P("cuts", None),
        P(None, ("dp", "cuts")),
    )
    return jax.shard_map(
        on_device,
        mesh=mesh,
        in_specs=placed,
        out_specs=P(("dp", "cuts"), "groups"),
        check_vma=False,
    )
```

time: 90 us -> 31.3 us (0.35)
  waiting for transfers between devices: 57.4 us -> 11.6 us
  between operations: 13.5 us -> 0.09 us
  starting transfers between devices: 7.03 us -> 13.1 us
  blocking collectives: 3.8 us -> 0 us
  Pallas kernels: 0 us -> 2.08 us
  local copies, waits for them, and re-layouts: 3.45 us -> 1.42 us
  other arithmetic: 2.51 us -> 1.21 us
    reduce_scatter x1 -> x0, waiting for transfers between devices: 52.9 us -> none  [on_device(): lax.psum_scatter(partial_value, ('dp', 'cuts'), scatter_dimension=0, tile...]
    ppermute x0 -> x4, waiting for transfers between devices: none -> 11.6 us  [exchange(): return lax.ppermute(value, axis, [(i, i ^ bit) for i in range(count)])]
    ppermute x0 -> x4, starting transfers between devices: none -> 8.15 us  [exchange(): return lax.ppermute(value, axis, [(i, i ^ bit) for i in range(count)])]
    all_to_all x1, waiting for transfers between devices: 4.56 us -> 0.01 us  [on_device(): lax.all_to_all(queries, ('dp', 'cuts'), split_axis=0, concat_axis=0, tile...]
    psum x1 -> x0, blocking collectives: 3.8 us -> none  [on_device(): inward, outward = lax.psum((inward_part, outward_part), 'cuts')]
    pallas_call x0 -> x1, Pallas kernels: none -> 2.08 us  [score(): pl.pallas_call(lambda *refs: score_kernel(row_count, rank, *refs), grid=(...]
    sort x1 -> x0, other arithmetic: 2.03 us -> none  [on_device(): inverse = jnp.argsort(doc_slots)]
    all_to_all x1, starting transfers between devices: 6.99 us -> 4.98 us  [on_device(): lax.all_to_all(queries, ('dp', 'cuts'), split_axis=0, concat_axis=0, tile...]
  transfers between devices with their start and end apart: 2 -> 5, of which waited for: 2 -> 2; matrix products, arithmetic and copies ran while one was open for 2% -> 1% of each run, Pallas kernels for 0% -> 0%
where the time goes in v1:
time: 31.3 us; the launch traced here: 31 us
  starting transfers between devices  13.1 us (42%)
  waiting for transfers between devices  11.6 us (37%)
  Pallas kernels  2.08 us (7%)
  matrix products  1.47 us (5%)
  local copies, waits for them, and re-layouts  1.42 us (5%)
  other arithmetic  1.21 us (4%)
    ppermute x4, waiting for transfers between devices, exchange(): return lax.ppermute(value, axis, [(i, i ^ bit) for i in range(count)])  11.6 us
    ppermute x4, starting transfers between devices, exchange(): return lax.ppermute(value, axis, [(i, i ^ bit) for i in range(count)])  8.15 us
    all_to_all x1, starting transfers between devices, on_device(): lax.all_to_all(queries, ('dp', 'cuts'), split_axis=0, concat_axis=0, tile...  4.98 us
    pallas_call x1, Pallas kernels, score(): pl.pallas_call(lambda *refs: score_kernel(row_count, rank, *refs), grid=(...  2.08 us
    unnamed x10, local copies, waits for them, and re-layouts  1.34 us
    dot_general x1, matrix products, on_device(): inward = jnp.dot(activations, proj_in, preferred_element_type=jnp.float32)  1.26 us
    broadcast_in_dim x1, other arithmetic, on_device(): jnp.where(member, 1.0 / tally.astype(jnp.float32)[None, :], 0.0)  0.71 us
  transfers between devices with their start and end apart: 5, of which 2 were waited for; matrix products, arithmetic and copies ran while one was open for 1% of the time, Pallas kernels for 0%

profile of v1, /device:TPU:0, one launch (start us, length us, event | category | flops | bytes accessed | tf_op | source)
XLA Modules:
  0.0 31.0 jit_solution(15448588880696497925)
XLA Ops:
  0.0 0.7 %divide_bitcast_fusion = f32[8]{0:T(128)S(1)} fusion(s32[1,8]{1,0:T(1,128)} %param.11), kind=kLoop, calls=%fused_computation.18 | loop fusion | flops 16 | bytes 64 | tf_op jit(solution)/shard_map/jit(_where)/broadcast_in_dim | solution.py:97
  0.7 0.7 %copy-done.3 = s32[1,8]{1,0:T(1,128)S(1)} copy-done((s32[1,8]{1,0:T(1,128)S(1)}, s32[1,8]{1,0:T(1,128)}, u32[]{:S(2)}) %copy-start.3) | copy-done | bytes 56
  1.4 0.1 select_reduce_fusion.2
  1.5 0.1 select_reduce_fusion.1
  1.6 0.0 copy-start.2
  1.6 1.3 %fusion.3 = f32[48,64]{1,0:T(8,128)S(1)} fusion(bf16[48,3584]{1,0:T(8,128)(2,1)} %param.9, bf16[3584,64]{0,1:T(8,128)(2,1)S(1)} %copy-done), kind=kOutput, calls=%fused_computation.19 | convolution fusion | flops 22020096 | bytes 815104 | tf_op jit(solution)/shard_map/dot_general | solution.py:89
  2.9 0.0 copy-done.1
  2.9 0.2 convolution_multiply_fusion
  3.1 0.1 pad_maximum_fusion.3
  3.2 0.5 %collective-permute-start = (f32[48,128]{1,0:T(8,128)S(1)}, f32[48,128]{1,0:T(8,128)S(1)}, u32[]{:S(2)}, u32[]{:S(2)}) collective-permute-start(f32[48,128]{1,0:T(8,128)S(1)} %pad_maximum_fusion.3), channel_id=1, source_target_pairs={{0,1},{1,0},{2,3},{3,2},{4,5},{5,4},{6,7},{7,6},{8,9},{9,8},{10,11... | collective-permute-start | bytes 73736 | tf_op jit(solution)/shard_map/ppermute | solution.py:71
  3.7 0.7 %copy-done.4 = s32[64]{0:T(128)S(1)} copy-done((s32[64]{0:T(128)S(1)}, s32[64]{0:T(128)}, u32[]{:S(2)}) %copy-start.4) | copy-done | bytes 280
  4.3 0.1 dynamic_slice.3
  4.4 0.1 select_reduce_fusion
  4.5 0.0 collective-permute-done
  4.5 0.1 fusion.8
  4.6 2.9 %collective-permute-start.1 = (f32[1,56,128]{2,1,0:T(8,128)S(1)}, f32[1,56,128]{2,1,0:T(8,128)S(1)}, u32[]{:S(2)}, u32[]{:S(2)}) collective-permute-start(f32[1,56,128]{2,1,0:T(8,128)S(1)} %fusion), channel_id=1, source_target_pairs={{0,2},{2,0},{4,6},{6,4},{8,10},{10,8},{12,14},{14,12},{1,3},{3,1},... | collective-permute-start | bytes 86024 | tf_op jit(solution)/shard_map/ppermute | solution.py:71
  7.5 5.0 %all-to-all-start = ((bf16[16,32,256]{2,1,0:T(8,128)(2,1)}), bf16[16,32,256]{2,1,0:T(8,128)(2,1)S(1)}, u32[]{:S(2)}, u32[]{:S(2)}) async-start(bf16[16,32,256]{2,1,0:T(8,128)(2,1)} %bitcast.6), calls=%async_computation | async-start | bytes 524288 | tf_op jit(solution)/shard_map/all_to_all | solution.py:84
  12.5 0.0 collective-permute-done.1
  12.5 2.0 %collective-permute-start.2 = (f32[2,56,128]{2,1,0:T(8,128)S(1)}, f32[2,56,128]{2,1,0:T(8,128)S(1)}, u32[]{:S(2)}, u32[]{:S(2)}) collective-permute-start(f32[2,56,128]{2,1,0:T(8,128)S(1)} %pad_maximum_fusion.2), channel_id=1, source_target_pairs={{0,4},{2,6},{4,0},{6,2},{8,12},{10,14},{12,8},{14,10},{1,5},{3,7},... | collective-permute-start | bytes 172040 | tf_op jit(solution)/shard_map/ppermute | solution.py:71
  14.5 6.2 %collective-permute-done.2 = f32[2,56,128]{2,1,0:T(8,128)S(1)} collective-permute-done((f32[2,56,128]{2,1,0:T(8,128)S(1)}, f32[2,56,128]{2,1,0:T(8,128)S(1)}, u32[]{:S(2)}, u32[]{:S(2)}) %collective-permute-start.2) | collective-permute-done | bytes 57376 | tf_op jit(solution)/shard_map/ppermute | solution.py:71
  20.7 2.8 %collective-permute-start.3 = (f32[4,56,128]{2,1,0:T(8,128)S(1)}, f32[4,56,128]{2,1,0:T(8,128)S(1)}, u32[]{:S(2)}, u32[]{:S(2)}) collective-permute-start(f32[4,56,128]{2,1,0:T(8,128)S(1)} %pad_maximum_fusion.1), channel_id=1, source_target_pairs={{0,8},{2,10},{4,12},{6,14},{8,0},{10,2},{12,4},{14,6},{1,9},{3,11}... | collective-permute-start | bytes 344072 | tf_op jit(solution)/shard_map/ppermute | solution.py:71
  23.5 5.4 %collective-permute-done.3 = f32[4,56,128]{2,1,0:T(8,128)S(1)} collective-permute-done((f32[4,56,128]{2,1,0:T(8,128)S(1)}, f32[4,56,128]{2,1,0:T(8,128)S(1)}, u32[]{:S(2)}, u32[]{:S(2)}) %collective-permute-start.3) | collective-permute-done | bytes 114720 | tf_op jit(solution)/shard_map/ppermute | solution.py:71
  28.9 0.0 all-to-all-done
  29.0 2.1 %score.1 = f32[32,64]{1,0:T(8,128)} custom-call(f32[8,56,128]{2,1,0:T(8,128)S(1)} %pad_maximum_fusion.refs_0_, bf16[512,256]{1,0:T(8,128)(2,1)S(1)} %bitcast.19), custom_call_target="tpu_custom_call" | custom-call | tf_op jit(solution)/shard_map/score/pallas_call | solution.py:55
  (12 shorter events, 0.1 us)
Async XLA Ops:
  0.0 1.6 %copy-start = (bf16[3584,64]{0,1:T(8,128)(2,1)S(1)}, bf16[3584,64]{0,1:T(8,128)(2,1)}, u32[]{:S(2)}) copy-start(bf16[3584,64]{0,1:T(8,128)(2,1)} %param.13) | copy-start | bytes 1376260
  0.7 0.7 %copy-start.3 = (s32[1,8]{1,0:T(1,128)S(1)}, s32[1,8]{1,0:T(1,128)}, u32[]{:S(2)}) copy-start(s32[1,8]{1,0:T(1,128)} %param.11) | copy-start | bytes 100
  1.6 1.3 %copy-start.1 = (bf16[2048,64]{0,1:T(8,128)(2,1)S(1)}, bf16[2048,64]{0,1:T(8,128)(2,1)}, u32[]{:S(2)}) copy-start(bf16[2048,64]{0,1:T(8,128)(2,1)} %param.14) | copy-start | bytes 786436
  1.6 1.3 %copy-start.2 = (bf16[48,2048]{1,0:T(8,128)(2,1)S(1)}, bf16[48,2048]{1,0:T(8,128)(2,1)}, u32[]{:S(2)}) copy-start(bf16[48,2048]{1,0:T(8,128)(2,1)} %param.10) | copy-start | bytes 589828
  3.2 1.3 %collective-permute-start = (f32[48,128]{1,0:T(8,128)S(1)}, f32[48,128]{1,0:T(8,128)S(1)}, u32[]{:S(2)}, u32[]{:S(2)}) collective-permute-start(f32[48,128]{1,0:T(8,128)S(1)} %pad_maximum_fusion.3), channel_id=1, source_target_pairs={{0,1},{1,0},{2,3},{3,2},{4,5},{5,4},{6,7},{7,6},{8,9},{9,8},{10,11... | collective-permute-start | bytes 73736 | tf_op jit(solution)/shard_map/ppermute | solution.py:71
  3.7 0.7 %copy-start.4 = (s32[64]{0:T(128)S(1)}, s32[64]{0:T(128)}, u32[]{:S(2)}) copy-start(s32[64]{0:T(128)} %param.12) | copy-start | bytes 772
  4.6 7.9 %collective-permute-start.1 = (f32[1,56,128]{2,1,0:T(8,128)S(1)}, f32[1,56,128]{2,1,0:T(8,128)S(1)}, u32[]{:S(2)}, u32[]{:S(2)}) collective-permute-start(f32[1,56,128]{2,1,0:T(8,128)S(1)} %fusion), channel_id=1, source_target_pairs={{0,2},{2,0},{4,6},{6,4},{8,10},{10,8},{12,14},{14,12},{1,3},{3,1},... | collective-permute-start | bytes 86024 | tf_op jit(solution)/shard_map/ppermute | solution.py:71
  7.5 21.4 %all-to-all-start = ((bf16[16,32,256]{2,1,0:T(8,128)(2,1)}), bf16[16,32,256]{2,1,0:T(8,128)(2,1)S(1)}, u32[]{:S(2)}, u32[]{:S(2)}) async-start(bf16[16,32,256]{2,1,0:T(8,128)(2,1)} %bitcast.6), calls=%async_computation | async-start | bytes 524288 | tf_op jit(solution)/shard_map/all_to_all | solution.py:84
  12.5 8.2 %collective-permute-start.2 = (f32[2,56,128]{2,1,0:T(8,128)S(1)}, f32[2,56,128]{2,1,0:T(8,128)S(1)}, u32[]{:S(2)}, u32[]{:S(2)}) collective-permute-start(f32[2,56,128]{2,1,0:T(8,128)S(1)} %pad_maximum_fusion.2), channel_id=1, source_target_pairs={{0,4},{2,6},{4,0},{6,2},{8,12},{10,14},{12,8},{14,10},{1,5},{3,7},... | collective-permute-start | bytes 172040 | tf_op jit(solution)/shard_map/ppermute | solution.py:71
  20.7 8.2 %collective-permute-start.3 = (f32[4,56,128]{2,1,0:T(8,128)S(1)}, f32[4,56,128]{2,1,0:T(8,128)S(1)}, u32[]{:S(2)}, u32[]{:S(2)}) collective-permute-start(f32[4,56,128]{2,1,0:T(8,128)S(1)} %pad_maximum_fusion.1), channel_id=1, source_target_pairs={{0,8},{2,10},{4,12},{6,14},{8,0},{10,2},{12,4},{14,6},{1,9},{3,11}... | collective-permute-start | bytes 344072 | tf_op jit(solution)/shard_map/ppermute | solution.py:71

commit v2 on v1

v2 whole, which is shorter than its diff:
```python
import functools
import math

import jax
import jax.numpy as jnp
from jax import lax
from jax.experimental import pallas as pl
from jax.experimental.pallas import tpu as pltpu
from jax.sharding import PartitionSpec as P

TILE = 8
LANES = 128


def project_kernel(*refs):
    sources, payload_ref, held, sem = refs[:6], refs[6], refs[7:13], refs[13]
    copies = [pltpu.make_async_copy(source, kept, sem.at[i]) for i, (source, kept) in enumerate(zip(sources, held))]
    for copy in copies:
        copy.start()
    acts_ref, in_ref, grads_ref, out_ref, counts_ref, slots_ref = held
    row_count = acts_ref.shape[0]
    rank = in_ref.shape[0]
    doc_count = counts_ref.shape[1]
    contract = (((1,), (1,)), ((), ()))
    row = lax.broadcasted_iota(jnp.int32, (row_count, rank), 0)
    lane = lax.broadcasted_iota(jnp.int32, (TILE, 2 * rank), 1)
    tally = jnp.ones((row_count, rank), jnp.int32)
    slots = jnp.zeros((TILE, 2 * rank), jnp.int32)
    first_doc = lax.axis_index("dp") * doc_count
    copies[4].wait()
    copies[5].wait()
    start = jnp.int32(0)
    for doc in range(doc_count):
        count = counts_ref[0, doc]
        tally = jnp.where((row >= start) & (row < start + count), count, tally)
        slots = jnp.where((lane >= start) & (lane < start + count), slots_ref[first_doc + doc], slots)
        start = start + count
    leader = (lax.axis_index("cuts") == 0).astype(jnp.float32)
    payload_ref[row_count:, :] = slots.astype(jnp.float32) * leader
    copies[0].wait()
    copies[1].wait()
    inward = lax.dot_general(acts_ref[...], in_ref[...], contract, preferred_element_type=jnp.float32)
    payload_ref[:row_count, :rank] = inward
    copies[2].wait()
    copies[3].wait()
    outward = lax.dot_general(grads_ref[...], out_ref[...], contract, preferred_element_type=jnp.float32)
    payload_ref[:row_count, rank:] = outward / tally.astype(jnp.float32)


def project(counts, doc_slots, activations, out_grads, proj_in, proj_out):
    row_count, rank = activations.shape[0], proj_in.shape[1]
    operands = (activations, proj_in.T, out_grads, proj_out.T, counts, doc_slots)
    spaces = [pltpu.VMEM] * 4 + [pltpu.SMEM] * 2
    return pl.pallas_call(
        project_kernel,
        in_specs=[pl.BlockSpec(memory_space=pltpu.HBM)] * len(operands),
        out_specs=pl.BlockSpec(memory_space=pltpu.VMEM),
        scratch_shapes=[space(operand.shape, operand.dtype) for space, operand in zip(spaces, operands)]
        + [pltpu.SemaphoreType.DMA((len(operands),))],
        out_shape=jax.ShapeDtypeStruct((row_count + TILE, 2 * rank), jnp.float32),
        compiler_params=pltpu.CompilerParams(vmem_limit_bytes=60 * 1024 * 1024),
        name="project",
    )(*operands)


def score_kernel(row_count, rank, origins, other, payload_ref, query_ref, scores_ref, outward_ref):
    sources = payload_ref.shape[0]
    query_rows, columns = scores_ref.shape
    chunks, halves = query_ref.shape[:2]
    split = query_ref.shape[3] // rank
    tokens = sources * row_count
    here = lax.axis_index("dp") * lax.axis_size("cuts") + lax.axis_index("cuts")
    parts = lax.axis_size("dp") * lax.axis_size("cuts")
    half = here // (parts // halves)
    target = halves - 1 - half if other else half
    payload = payload_ref[...]
    turned = payload[:, :row_count, :].reshape(tokens, 2 * rank).T
    inward = turned[:rank]
    outward_ref[...] = turned[rank:]
    high = inward.astype(jnp.bfloat16)
    low = (inward - high.astype(jnp.float32)).astype(jnp.bfloat16)
    blank = jnp.zeros_like(high)
    group = math.gcd(split, max(1, LANES // rank))
    total = jnp.zeros((query_rows, tokens), jnp.float32)
    for part in range(split):
        first = part // group * group
        query = query_ref[:, target, :, first * rank:(first + group) * rank].reshape(chunks * query_rows, group * rank)
        column = [blank] * (2 * group)
        column[part - first], column[part - first + group] = high, low
        met = jnp.dot(
            jnp.concatenate([query, query], axis=1),
            jnp.concatenate(column, axis=0),
            preferred_element_type=jnp.float32,
        )
        for chunk in range(chunks):
            origin = half * chunks + chunk if origins is None else here ^ origins[chunk]
            factor = outward_ref[pl.ds(origin * split + part, 1), :]
            total = total + met[chunk * query_rows:(chunk + 1) * query_rows] * factor
    marks = payload[:, row_count:, :].reshape(sources * TILE, 2 * rank).T
    slots = jnp.concatenate([marks[:row_count, s * TILE:s * TILE + 1] for s in range(sources)], axis=0)
    column_of = lax.broadcasted_iota(jnp.int32, (tokens, columns), 1)
    member = (slots.astype(jnp.int32) == column_of).astype(jnp.bfloat16)
    total_high = total.astype(jnp.bfloat16)
    total_low = (total - total_high.astype(jnp.float32)).astype(jnp.bfloat16)
    scores = jnp.dot(total_high, member, preferred_element_type=jnp.float32)
    scores = scores + jnp.dot(total_low, member, preferred_element_type=jnp.float32)

    @pl.when(pl.program_id(0) == 0)
    def _():
        scores_ref[...] = scores

    @pl.when(pl.program_id(0) > 0)
    def _():
        scores_ref[...] += scores


def score(payload, query, columns, row_count, rank, origins, other):
    sources = payload.shape[0]
    query_rows = query.shape[2]
    step = min(sources, 8)
    return pl.pallas_call(
        functools.partial(score_kernel, row_count, rank, origins, other),
        grid=(sources // step,),
        in_specs=[
            pl.BlockSpec((step,) + payload.shape[1:], lambda i: (i, 0, 0)),
            pl.BlockSpec(query.shape, lambda i: (0, 0, 0, 0)),
        ],
        out_specs=pl.BlockSpec((query_rows, columns), lambda i: (0, 0)),
        out_shape=jax.ShapeDtypeStruct((query_rows, columns), jnp.float32),
        scratch_shapes=[pltpu.VMEM((rank, step * row_count), jnp.float32)],
        compiler_params=pltpu.CompilerParams(vmem_limit_bytes=48 * 1024 * 1024),
        name="score_other" if other else "score_own",
    )(payload, query)


def exchange(value, axis, bit):
    count = lax.axis_size(axis)
    return lax.ppermute(value, axis, [(i, i ^ bit) for i in range(count)])


def on_device(activations, out_grads, counts, doc_slots, proj_in, proj_out, queries):
    row_count = activations.shape[0]
    rank = proj_in.shape[1]
    both = ("dp", "cuts")
    cut_count = lax.axis_size("cuts")
    data_count = lax.axis_size("dp")
    parts = cut_count * data_count
    query_rows = queries.shape[0] // parts
    width = queries.shape[1]

    here = lax.axis_index(both)
    arrived = queries.reshape(1, 2, parts // 2, query_rows, width)
    origins = [0]
    steps = []
    bit = parts // 4
    while bit > 0:
        sides = arrived.reshape(arrived.shape[0], 2, 2, bit, query_rows, width)
        side = (here // bit) % 2
        leaving = lax.dynamic_index_in_dim(sides, 1 - side, 2, keepdims=False)
        staying = lax.dynamic_index_in_dim(sides, side, 2, keepdims=False)
        landed = exchange(leaving, both, bit)
        steps.append(landed)
        if width % rank:
            pair = (jnp.where(side == 0, staying, landed), jnp.where(side == 0, landed, staying))
            arrived = jnp.stack(pair, axis=1).reshape((-1,) + staying.shape[1:])
        else:
            arrived = jnp.concatenate([staying, landed], axis=0)
        origins = origins + [origin ^ bit for origin in origins]
        bit //= 2
    arrived = arrived.reshape(parts // 2, 2, query_rows, width)
    if width % rank:
        arrived = arrived.transpose(1, 2, 0, 3).reshape(2, query_rows, -1, rank).transpose(2, 0, 1, 3)
        origins = None

    payload = project(counts, doc_slots, activations, out_grads, proj_in, proj_out)
    bit = 1
    while bit < cut_count:
        payload = payload + exchange(payload, "cuts", bit)
        bit *= 2
    payload = payload[None]
    bit = data_count // 2
    while bit > 0:
        payload = jnp.concatenate([payload, exchange(payload, "dp", bit)], axis=0)
        bit //= 2
    columns = doc_slots.shape[0]
    theirs = score(payload, arrived, columns, row_count, rank, origins, True)
    own = score(payload, arrived, columns, row_count, rank, origins, False)
    return own + exchange(theirs, both, parts // 2)


def solution(mesh):
    placed = (
        P(("groups", "dp"), "cuts"),
        P(("groups", "dp"), "cuts"),
        P(("groups", "dp"), None),
        P("groups"),
        P("cuts", None),
        P("cuts", None),
        P(None, ("dp", "cuts")),
    )
    return jax.shard_map(
        on_device,
        mesh=mesh,
        in_specs=placed,
        out_specs=P(("dp", "cuts"), "groups"),
        check_vma=False,
    )
```

time: 31.3 us -> 26.8 us (0.86)
  Pallas kernels: 2.08 us -> 3.81 us
  waiting for transfers between devices: 11.6 us -> 10 us
  matrix products: 1.47 us -> 0 us
  local copies, waits for them, and re-layouts: 1.42 us -> 0.05 us
  starting transfers between devices: 13.1 us -> 12 us
  other arithmetic: 1.21 us -> 0.73 us
    all_to_all x1 -> x0, starting transfers between devices: 4.98 us -> none  [on_device(): lax.all_to_all(queries, ('dp', 'cuts'), split_axis=0, concat_axis=0, tile...]
    ppermute x4 -> x8, starting transfers between devices: 8.15 us -> 12 us  [exchange(): return lax.ppermute(value, axis, [(i, i ^ bit) for i in range(count)])]
    pallas_call x1 -> x3, Pallas kernels: 2.08 us -> 3.81 us  [the longest x1 2.48 us: project(): pl.pallas_call(project_kernel, in_specs=[pl.BlockSpec(memory_space=pltpu....]
    ppermute x4 -> x8, waiting for transfers between devices: 11.6 us -> 10 us  [exchange(): return lax.ppermute(value, axis, [(i, i ^ bit) for i in range(count)])]
    dot_general x2 -> x0, matrix products: 1.47 us -> none  [the longest x1 1.26 us: on_device(): inward = jnp.dot(activations, proj_in, preferred_element_type=jnp.float32)]
    unnamed x10 -> x4, local copies, waits for them, and re-layouts: 1.34 us -> 0.01 us
    broadcast_in_dim x2 -> x1, other arithmetic: 0.72 us -> 0.01 us  [on_device(): payload = payload[None]]
    add x1, other arithmetic: 0.08 us -> 0.61 us  [on_device(): return own + exchange(theirs, both, parts // 2)]
  transfers between devices with their start and end apart: 5 -> 8, of which waited for: 2 -> 7; matrix products, arithmetic and copies ran while one was open for 1% -> 0% of each run, Pallas kernels for 0% -> 2%
where the time goes in v2:
time: 26.8 us; the launch traced here: 26.6 us
  starting transfers between devices  12 us (45%)
  waiting for transfers between devices  10 us (37%)
  Pallas kernels  3.81 us (14%)
  other arithmetic  0.73 us (3%)
    ppermute x8, starting transfers between devices, exchange(): return lax.ppermute(value, axis, [(i, i ^ bit) for i in range(count)])  12 us
    ppermute x8, waiting for transfers between devices, exchange(): return lax.ppermute(value, axis, [(i, i ^ bit) for i in range(count)])  10 us
    pallas_call x1, Pallas kernels, project(): pl.pallas_call(project_kernel, in_specs=[pl.BlockSpec(memory_space=pltpu....  2.48 us
    pallas_call x2, Pallas kernels, score(): pl.pallas_call(functools.partial(score_kernel, row_count, rank, origins,...  1.32 us
    add x1, other arithmetic, on_device(): return own + exchange(theirs, both, parts // 2)  0.61 us
  transfers between devices with their start and end apart: 8, of which 7 were waited for; matrix products, arithmetic and copies ran while one was open for 0% of the time, Pallas kernels for 2%

profile of v2, /device:TPU:0, one launch (start us, length us, event | category | flops | bytes accessed | tf_op | source)
XLA Modules:
  0.0 26.6 jit_solution(11051870198271792218)
XLA Ops:
  0.0 0.0 copy-start
  0.0 2.5 %project.1 = f32[56,128]{1,0:T(8,128)} custom-call(bf16[48,3584]{1,0:T(8,128)(2,1)} %refs_0_.1, bf16[64,3584]{1,0:T(8,128)(2,1)} %bitcast.19, bf16[48,2048]{1,0:T(8,128)(2,1)} %refs_2_.1, bf16[64,2048]{1,0:T(8,128)(2,1)} %bitcast.21, s32[1,8]{1,0:T(1,128)} %refs_4_.1, s32[64]{0:T(128)} %refs_5_.1), custom_call_target="tpu_custom_call" | custom-call | tf_op jit(solution)/shard_map/project/pallas_call | solution.py:54
  2.5 0.5 %collective-permute-start = (f32[56,128]{1,0:T(8,128)}, f32[56,128]{1,0:T(8,128)S(1)}, u32[]{:S(2)}, u32[]{:S(2)}) collective-permute-start(f32[56,128]{1,0:T(8,128)} %project.1), channel_id=1, source_target_pairs={{0,1},{1,0},{2,3},{3,2},{4,5},{5,4},{6,7},{7,6},{8,9},{9,8},{10,11... | collective-permute-start | bytes 86024 | tf_op jit(solution)/shard_map/ppermute | solution.py:138
  3.0 0.0 copy-start.1
  3.0 1.1 %collective-permute-done = f32[56,128]{1,0:T(8,128)S(1)} collective-permute-done((f32[56,128]{1,0:T(8,128)}, f32[56,128]{1,0:T(8,128)S(1)}, u32[]{:S(2)}, u32[]{:S(2)}) %collective-permute-start) | collective-permute-done | bytes 28704 | tf_op jit(solution)/shard_map/ppermute | solution.py:138
  4.1 0.0 copy-done.1
  4.1 4.0 %collective-permute-start.1 = (f32[1,56,128]{2,1,0:T(8,128)S(1)}, f32[1,56,128]{2,1,0:T(8,128)S(1)}, u32[]{:S(2)}, u32[]{:S(2)}) collective-permute-start(f32[1,56,128]{2,1,0:T(8,128)S(1)} %add_bitcast_fusion), channel_id=1, source_target_pairs={{0,8},{2,10},{4,12},{6,14},{8,0},{10,2},{12,4},{14,6},{1,9},{3,11}... | collective-permute-start | bytes 86024 | tf_op jit(solution)/shard_map/ppermute | solution.py:138
  8.1 0.0 copy-done
  8.1 1.6 %collective-permute-start.4 = (bf16[1,2,4,32,256]{4,3,2,1,0:T(8,128)(2,1)S(1)}, bf16[1,2,4,32,256]{4,3,2,1,0:T(8,128)(2,1)S(1)}, u32[]{:S(2)}, u32[]{:S(2)}) collective-permute-start(bf16[1,2,4,32,256]{4,3,2,1,0:T(8,128)(2,1)S(1)} %get-tuple-element.9), channel_id=1, source_target_pairs={{0,4},{1,5},{2,6},{3,7},{4,0},{5,1},{6,2},{7,3},{8,12},{9,13},{10,... | collective-permute-start | bytes 393224 | tf_op jit(solution)/shard_map/ppermute | solution.py:138
  9.8 0.2 collective-permute-done.1
  9.9 2.2 %collective-permute-start.2 = (f32[2,56,128]{2,1,0:T(8,128)S(1)}, f32[2,56,128]{2,1,0:T(8,128)S(1)}, u32[]{:S(2)}, u32[]{:S(2)}) collective-permute-start(f32[2,56,128]{2,1,0:T(8,128)S(1)} %pad_maximum_fusion.2), channel_id=1, source_target_pairs={{0,4},{2,6},{4,0},{6,2},{8,12},{10,14},{12,8},{14,10},{1,5},{3,7},... | collective-permute-start | bytes 172040 | tf_op jit(solution)/shard_map/ppermute | solution.py:138
  12.1 1.9 %collective-permute-done.4 = bf16[1,2,4,32,256]{4,3,2,1,0:T(8,128)(2,1)S(1)} collective-permute-done((bf16[1,2,4,32,256]{4,3,2,1,0:T(8,128)(2,1)S(1)}, bf16[1,2,4,32,256]{4,3,2,1,0:T(8,128)(2,1)S(1)}, u32[]{:S(2)}, u32[]{:S(2)}) %collective-permute-start.4) | collective-permute-done | bytes 131104 | tf_op jit(solution)/shard_map/ppermute | solution.py:138
  14.1 1.6 %collective-permute-start.5 = (bf16[2,2,2,32,256]{4,3,1,0,2:T(8,128)(2,1)S(1)}, bf16[2,2,2,32,256]{4,3,1,0,2:T(8,128)(2,1)S(1)}, u32[]{:S(2)}, u32[]{:S(2)}) collective-permute-start(bf16[2,2,2,32,256]{4,3,1,0,2:T(8,128)(2,1)S(1)} %bitcast.22), channel_id=1, source_target_pairs={{0,2},{1,3},{2,0},{3,1},{4,6},{5,7},{6,4},{7,5},{8,10},{9,11},{10,... | collective-permute-start | bytes 393224 | tf_op jit(solution)/shard_map/ppermute | solution.py:138
  15.7 0.0 collective-permute-done.2
  15.7 0.6 %collective-permute-start.3 = (f32[4,56,128]{2,1,0:T(8,128)S(1)}, f32[4,56,128]{2,1,0:T(8,128)S(1)}, u32[]{:S(2)}, u32[]{:S(2)}) collective-permute-start(f32[4,56,128]{2,1,0:T(8,128)S(1)} %pad_maximum_fusion.1), channel_id=1, source_target_pairs={{0,2},{2,0},{4,6},{6,4},{8,10},{10,8},{12,14},{14,12},{1,3},{3,1},... | collective-permute-start | bytes 344072 | tf_op jit(solution)/shard_map/ppermute | solution.py:138
  16.3 2.9 %collective-permute-done.5 = bf16[2,2,2,32,256]{4,3,1,0,2:T(8,128)(2,1)S(1)} collective-permute-done((bf16[2,2,2,32,256]{4,3,1,0,2:T(8,128)(2,1)S(1)}, bf16[2,2,2,32,256]{4,3,1,0,2:T(8,128)(2,1)S(1)}, u32[]{:S(2)}, u32[]{:S(2)}) %collective-permute-start.5) | collective-permute-done | bytes 131104 | tf_op jit(solution)/shard_map/ppermute | solution.py:138
  19.2 0.1 collective-permute-start.6
  19.3 1.2 %collective-permute-done.3 = f32[4,56,128]{2,1,0:T(8,128)S(1)} collective-permute-done((f32[4,56,128]{2,1,0:T(8,128)S(1)}, f32[4,56,128]{2,1,0:T(8,128)S(1)}, u32[]{:S(2)}, u32[]{:S(2)}) %collective-permute-start.3) | collective-permute-done | bytes 114720 | tf_op jit(solution)/shard_map/ppermute | solution.py:138
  20.6 0.1 collective-permute-done.6
  20.7 0.7 %score_other.1 = f32[32,64]{1,0:T(8,128)S(1)} custom-call(f32[8,56,128]{2,1,0:T(8,128)S(1)} %pad_maximum_fusion.payload_ref, bf16[8,2,32,256]{3,2,1,0:T(8,128)(2,1)S(1)} %maximum_bitcast_fusion.query_ref), custom_call_target="tpu_custom_call" | custom-call | tf_op jit(solution)/shard_map/score_other/pallas_call | solution.py:121
  21.3 1.4 %collective-permute-start.7 = (f32[32,64]{1,0:T(8,128)S(1)}, f32[32,64]{1,0:T(8,128)S(1)}, u32[]{:S(2)}, u32[]{:S(2)}) collective-permute-start(f32[32,64]{1,0:T(8,128)S(1)} %score_other.1), channel_id=1, source_target_pairs={{0,8},{1,9},{2,10},{3,11},{4,12},{5,13},{6,14},{7,15},{8,0},{9,1},... | collective-permute-start | bytes 24584 | tf_op jit(solution)/shard_map/ppermute | solution.py:138
  22.7 0.7 %score_own.1 = f32[32,64]{1,0:T(8,128)S(1)} custom-call(f32[8,56,128]{2,1,0:T(8,128)S(1)} %pad_maximum_fusion.payload_ref, bf16[8,2,32,256]{3,2,1,0:T(8,128)(2,1)S(1)} %maximum_bitcast_fusion.query_ref), custom_call_target="tpu_custom_call" | custom-call | tf_op jit(solution)/shard_map/score_own/pallas_call | solution.py:121
  23.4 2.7 %collective-permute-done.7 = f32[32,64]{1,0:T(8,128)S(1)} collective-permute-done((f32[32,64]{1,0:T(8,128)S(1)}, f32[32,64]{1,0:T(8,128)S(1)}, u32[]{:S(2)}, u32[]{:S(2)}) %collective-permute-start.7) | collective-permute-done | bytes 8224 | tf_op jit(solution)/shard_map/ppermute | solution.py:138
  26.0 0.6 %add.57 = f32[32,64]{1,0:T(8,128)} add(f32[32,64]{1,0:T(8,128)S(1)} %score_own.1, f32[32,64]{1,0:T(8,128)S(1)} %collective-permute-done.7) | non-fusion elementwise | flops 2048 | bytes 24576 | tf_op jit(solution)/shard_map/add | solution.py:188
  (10 shorter events, 0.2 us)
Async XLA Ops:
  0.0 8.1 %copy-start = (bf16[512,256]{1,0:T(8,128)(2,1)S(1)}, bf16[512,256]{1,0:T(8,128)(2,1)}, u32[]{:S(2)}) copy-start(bf16[512,256]{1,0:T(8,128)(2,1)} %param.13) | copy-start | bytes 786436
  2.5 1.6 %collective-permute-start = (f32[56,128]{1,0:T(8,128)}, f32[56,128]{1,0:T(8,128)S(1)}, u32[]{:S(2)}, u32[]{:S(2)}) collective-permute-start(f32[56,128]{1,0:T(8,128)} %project.1), channel_id=1, source_target_pairs={{0,1},{1,0},{2,3},{3,2},{4,5},{5,4},{6,7},{7,6},{8,9},{9,8},{10,11... | collective-permute-start | bytes 86024 | tf_op jit(solution)/shard_map/ppermute | solution.py:138
  3.0 1.1 %copy-start.1 = (f32[56,128]{1,0:T(8,128)S(1)}, f32[56,128]{1,0:T(8,128)}, u32[]{:S(2)}) copy-start(f32[56,128]{1,0:T(8,128)} %project.1) | copy-start | bytes 86020
  4.1 5.8 %collective-permute-start.1 = (f32[1,56,128]{2,1,0:T(8,128)S(1)}, f32[1,56,128]{2,1,0:T(8,128)S(1)}, u32[]{:S(2)}, u32[]{:S(2)}) collective-permute-start(f32[1,56,128]{2,1,0:T(8,128)S(1)} %add_bitcast_fusion), channel_id=1, source_target_pairs={{0,8},{2,10},{4,12},{6,14},{8,0},{10,2},{12,4},{14,6},{1,9},{3,11}... | collective-permute-start | bytes 86024 | tf_op jit(solution)/shard_map/ppermute | solution.py:138
  8.1 6.0 %collective-permute-start.4 = (bf16[1,2,4,32,256]{4,3,2,1,0:T(8,128)(2,1)S(1)}, bf16[1,2,4,32,256]{4,3,2,1,0:T(8,128)(2,1)S(1)}, u32[]{:S(2)}, u32[]{:S(2)}) collective-permute-start(bf16[1,2,4,32,256]{4,3,2,1,0:T(8,128)(2,1)S(1)} %get-tuple-element.9), channel_id=1, source_target_pairs={{0,4},{1,5},{2,6},{3,7},{4,0},{5,1},{6,2},{7,3},{8,12},{9,13},{10,... | collective-permute-start | bytes 393224 | tf_op jit(solution)/shard_map/ppermute | solution.py:138
  9.9 5.7 %collective-permute-start.2 = (f32[2,56,128]{2,1,0:T(8,128)S(1)}, f32[2,56,128]{2,1,0:T(8,128)S(1)}, u32[]{:S(2)}, u32[]{:S(2)}) collective-permute-start(f32[2,56,128]{2,1,0:T(8,128)S(1)} %pad_maximum_fusion.2), channel_id=1, source_target_pairs={{0,4},{2,6},{4,0},{6,2},{8,12},{10,14},{12,8},{14,10},{1,5},{3,7},... | collective-permute-start | bytes 172040 | tf_op jit(solution)/shard_map/ppermute | solution.py:138
  14.1 5.1 %collective-permute-start.5 = (bf16[2,2,2,32,256]{4,3,1,0,2:T(8,128)(2,1)S(1)}, bf16[2,2,2,32,256]{4,3,1,0,2:T(8,128)(2,1)S(1)}, u32[]{:S(2)}, u32[]{:S(2)}) collective-permute-start(bf16[2,2,2,32,256]{4,3,1,0,2:T(8,128)(2,1)S(1)} %bitcast.22), channel_id=1, source_target_pairs={{0,2},{1,3},{2,0},{3,1},{4,6},{5,7},{6,4},{7,5},{8,10},{9,11},{10,... | collective-permute-start | bytes 393224 | tf_op jit(solution)/shard_map/ppermute | solution.py:138
  15.7 4.9 %collective-permute-start.3 = (f32[4,56,128]{2,1,0:T(8,128)S(1)}, f32[4,56,128]{2,1,0:T(8,128)S(1)}, u32[]{:S(2)}, u32[]{:S(2)}) collective-permute-start(f32[4,56,128]{2,1,0:T(8,128)S(1)} %pad_maximum_fusion.1), channel_id=1, source_target_pairs={{0,2},{2,0},{4,6},{6,4},{8,10},{10,8},{12,14},{14,12},{1,3},{3,1},... | collective-permute-start | bytes 344072 | tf_op jit(solution)/shard_map/ppermute | solution.py:138
  19.2 1.4 %collective-permute-start.6 = (bf16[4,2,1,32,256]{4,3,1,0,2:T(8,128)(2,1)S(1)}, bf16[4,2,1,32,256]{4,3,1,0,2:T(8,128)(2,1)S(1)}, u32[]{:S(2)}, u32[]{:S(2)}) collective-permute-start(bf16[4,2,1,32,256]{4,3,1,0,2:T(8,128)(2,1)S(1)} %get-tuple-element.6), channel_id=1, source_target_pairs={{0,1},{1,0},{2,3},{3,2},{4,5},{5,4},{6,7},{7,6},{8,9},{9,8},{10,11... | collective-permute-start | bytes 393224 | tf_op jit(solution)/shard_map/ppermute | solution.py:138
  21.3 4.7 %collective-permute-start.7 = (f32[32,64]{1,0:T(8,128)S(1)}, f32[32,64]{1,0:T(8,128)S(1)}, u32[]{:S(2)}, u32[]{:S(2)}) collective-permute-start(f32[32,64]{1,0:T(8,128)S(1)} %score_other.1), channel_id=1, source_target_pairs={{0,8},{1,9},{2,10},{3,11},{4,12},{5,13},{6,14},{7,15},{8,0},{9,1},... | collective-permute-start | bytes 24584 | tf_op jit(solution)/shard_map/ppermute | solution.py:138

commit v3 on v2

--- a/solution.py
+++ b/solution.py
@@ -15,8 +15,8 @@
 def project_kernel(*refs):
     sources, payload_ref, held, sem = refs[:6], refs[6], refs[7:13], refs[13]
     copies = [pltpu.make_async_copy(source, kept, sem.at[i]) for i, (source, kept) in enumerate(zip(sources, held))]
-    for copy in copies:
-        copy.start()
+    for i in (4, 5, 2, 3, 0, 1):
+        copies[i].start()
     acts_ref, in_ref, grads_ref, out_ref, counts_ref, slots_ref = held
     row_count = acts_ref.shape[0]
     rank = in_ref.shape[0]
@@ -37,14 +37,14 @@
         start = start + count
     leader = (lax.axis_index("cuts") == 0).astype(jnp.float32)
     payload_ref[row_count:, :] = slots.astype(jnp.float32) * leader
+    copies[2].wait()
+    copies[3].wait()
+    outward = lax.dot_general(grads_ref[...], out_ref[...], contract, preferred_element_type=jnp.float32)
+    payload_ref[:row_count, rank:] = outward / tally.astype(jnp.float32)
     copies[0].wait()
     copies[1].wait()
     inward = lax.dot_general(acts_ref[...], in_ref[...], contract, preferred_element_type=jnp.float32)
     payload_ref[:row_count, :rank] = inward
-    copies[2].wait()
-    copies[3].wait()
-    outward = lax.dot_general(grads_ref[...], out_ref[...], contract, preferred_element_type=jnp.float32)
-    payload_ref[:row_count, rank:] = outward / tally.astype(jnp.float32)
 
 
 def project(counts, doc_slots, activations, out_grads, proj_in, proj_out):
@@ -138,38 +138,50 @@
     return lax.ppermute(value, axis, [(i, i ^ bit) for i in range(count)])
 
 
+def pick(value, index, axis):
+    return lax.dynamic_index_in_dim(value, index, axis, keepdims=False)
+
+
 def on_device(activations, out_grads, counts, doc_slots, proj_in, proj_out, queries):
     row_count = activations.shape[0]
     rank = proj_in.shape[1]
     both = ("dp", "cuts")
     cut_count = lax.axis_size("cuts")
-    data_count = lax.axis_size("dp")
-    parts = cut_count * data_count
+    parts = cut_count * lax.axis_size("dp")
     query_rows = queries.shape[0] // parts
     width = queries.shape[1]
 
+    flip = cut_count - 1
     here = lax.axis_index(both)
-    arrived = queries.reshape(1, 2, parts // 2, query_rows, width)
+    half = here // (parts // 2)
+    bits = [1 << place for place in range((parts // 2 - 1).bit_length())]
+    order = [bit for bit in bits if bit >= cut_count] + [bit for bit in bits if bit < cut_count]
+    waiting = bits[::-1]
+    arrived = queries.reshape([1, 2] + [2] * len(bits) + [query_rows, width])
     origins = [0]
-    steps = []
-    bit = parts // 4
-    while bit > 0:
-        sides = arrived.reshape(arrived.shape[0], 2, 2, bit, query_rows, width)
-        side = (here // bit) % 2
-        leaving = lax.dynamic_index_in_dim(sides, 1 - side, 2, keepdims=False)
-        staying = lax.dynamic_index_in_dim(sides, side, 2, keepdims=False)
+    for bit in order:
+        place = 1 + waiting.index(bit)
+        waiting.remove(bit)
+        own = (here // bit) % 2
+        if bit >= cut_count:
+            leaving, staying = pick(arrived, 1 - own, place + 1), pick(arrived, own, place + 1)
+        else:
+            sides = [jnp.where(half == top, own, 1 - own) for top in range(2)]
+            leaving = jnp.stack([pick(arrived[:, top], 1 - sides[top], place) for top in range(2)], axis=1)
+            staying = jnp.stack([pick(arrived[:, top], sides[top], place) for top in range(2)], axis=1)
         landed = exchange(leaving, both, bit)
-        steps.append(landed)
         if width % rank:
-            pair = (jnp.where(side == 0, staying, landed), jnp.where(side == 0, landed, staying))
+            pair = (jnp.where(own == 0, staying, landed), jnp.where(own == 0, landed, staying))
             arrived = jnp.stack(pair, axis=1).reshape((-1,) + staying.shape[1:])
         else:
             arrived = jnp.concatenate([staying, landed], axis=0)
         origins = origins + [origin ^ bit for origin in origins]
-        bit //= 2
     arrived = arrived.reshape(parts // 2, 2, query_rows, width)
     if width % rank:
-        arrived = arrived.transpose(1, 2, 0, 3).reshape(2, query_rows, -1, rank).transpose(2, 0, 1, 3)
+        arrived = arrived.reshape([2] * len(bits) + [2, query_rows, width])
+        axes = [order.index(bit) for bit in bits[::-1]]
+        arrived = arrived.transpose([len(bits), len(bits) + 1] + axes + [len(bits) + 2])
+        arrived = arrived.reshape(2, query_rows, -1, rank).transpose(2, 0, 1, 3)
         origins = None
 
     payload = project(counts, doc_slots, activations, out_grads, proj_in, proj_out)
@@ -178,14 +190,13 @@
         payload = payload + exchange(payload, "cuts", bit)
         bit *= 2
     payload = payload[None]
-    bit = data_count // 2
-    while bit > 0:
-        payload = jnp.concatenate([payload, exchange(payload, "dp", bit)], axis=0)
-        bit //= 2
+    far = [bit for bit in bits + [parts // 2] if bit >= cut_count]
+    for bit in far[-2:] + far[-3::-1]:
+        payload = jnp.concatenate([payload, exchange(payload, both, bit ^ flip)], axis=0)
     columns = doc_slots.shape[0]
     theirs = score(payload, arrived, columns, row_count, rank, origins, True)
     own = score(payload, arrived, columns, row_count, rank, origins, False)
-    return own + exchange(theirs, both, parts // 2)
+    return own + exchange(theirs, both, parts // 2 ^ flip)
 
 
 def solution(mesh):

time: 26.8 us -> 24.7 us (0.922)
  waiting for transfers between devices: 10 us -> 6.64 us
  starting transfers between devices: 12 us -> 13.4 us
    ppermute x8, waiting for transfers between devices: 10 us -> 6.64 us  [exchange(): return lax.ppermute(value, axis, [(i, i ^ bit) for i in range(count)])]
    ppermute x8, starting transfers between devices: 12 us -> 13.4 us  [exchange(): return lax.ppermute(value, axis, [(i, i ^ bit) for i in range(count)])]
  transfers between devices with their start and end apart: 8 -> 8, of which waited for: 7 -> 7; matrix products, arithmetic and copies ran while one was open for 0% -> 1% of each run, Pallas kernels for 2% -> 3%
where the time goes in v3:
time: 24.7 us; the launch traced here: 24.6 us
  starting transfers between devices  13.4 us (54%)
  waiting for transfers between devices  6.64 us (27%)
  Pallas kernels  3.73 us (15%)
  other arithmetic  0.76 us (3%)
    ppermute x8, starting transfers between devices, exchange(): return lax.ppermute(value, axis, [(i, i ^ bit) for i in range(count)])  13.4 us
    ppermute x8, waiting for transfers between devices, exchange(): return lax.ppermute(value, axis, [(i, i ^ bit) for i in range(count)])  6.64 us
    pallas_call x1, Pallas kernels, project(): pl.pallas_call(project_kernel, in_specs=[pl.BlockSpec(memory_space=pltpu....  2.41 us
    pallas_call x2, Pallas kernels, score(): pl.pallas_call(functools.partial(score_kernel, row_count, rank, origins,...  1.32 us
    add x1, other arithmetic, on_device(): return own + exchange(theirs, both, parts // 2 ^ flip)  0.61 us
  transfers between devices with their start and end apart: 8, of which 7 were waited for; matrix products, arithmetic and copies ran while one was open for 1% of the time, Pallas kernels for 3%

profile of v3, /device:TPU:0, one launch (start us, length us, event | category | flops | bytes accessed | tf_op | source)
XLA Modules:
  0.0 24.6 jit_solution(3640580411065792759)
XLA Ops:
  0.0 0.0 copy-start
  0.0 2.4 %project.1 = f32[56,128]{1,0:T(8,128)} custom-call(bf16[48,3584]{1,0:T(8,128)(2,1)} %refs_0_.1, bf16[64,3584]{1,0:T(8,128)(2,1)} %bitcast.21, bf16[48,2048]{1,0:T(8,128)(2,1)} %refs_2_.1, bf16[64,2048]{1,0:T(8,128)(2,1)} %bitcast.23, s32[1,8]{1,0:T(1,128)} %refs_4_.1, s32[64]{0:T(128)} %refs_5_.1), custom_call_target="tpu_custom_call" | custom-call | tf_op jit(solution)/shard_map/project/pallas_call | solution.py:54
  2.4 0.5 %collective-permute-start = (f32[56,128]{1,0:T(8,128)}, f32[56,128]{1,0:T(8,128)S(1)}, u32[]{:S(2)}, u32[]{:S(2)}) collective-permute-start(f32[56,128]{1,0:T(8,128)} %project.1), channel_id=1, source_target_pairs={{0,1},{1,0},{2,3},{3,2},{4,5},{5,4},{6,7},{7,6},{8,9},{9,8},{10,11... | collective-permute-start | bytes 86024 | tf_op jit(solution)/shard_map/ppermute | solution.py:138
  2.9 0.0 copy-start.1
  2.9 1.1 %collective-permute-done = f32[56,128]{1,0:T(8,128)S(1)} collective-permute-done((f32[56,128]{1,0:T(8,128)}, f32[56,128]{1,0:T(8,128)S(1)}, u32[]{:S(2)}, u32[]{:S(2)}) %collective-permute-start) | collective-permute-done | bytes 28704 | tf_op jit(solution)/shard_map/ppermute | solution.py:138
  4.0 0.0 copy-done.1
  4.0 2.7 %collective-permute-start.1 = (f32[1,56,128]{2,1,0:T(8,128)S(1)}, f32[1,56,128]{2,1,0:T(8,128)S(1)}, u32[]{:S(2)}, u32[]{:S(2)}) collective-permute-start(f32[1,56,128]{2,1,0:T(8,128)S(1)} %add_bitcast_fusion), channel_id=1, source_target_pairs={{0,5},{1,4},{2,7},{3,6},{4,1},{5,0},{6,3},{7,2},{8,13},{9,12},{10,... | collective-permute-start | bytes 86024 | tf_op jit(solution)/shard_map/ppermute | solution.py:138
  6.8 0.0 copy-done
  6.8 1.6 %collective-permute-start.4 = (bf16[1,2,2,2,32,256]{5,4,3,2,1,0:T(8,128)(2,1)S(1)}, bf16[1,2,2,2,32,256]{5,4,3,2,1,0:T(8,128)(2,1)S(1)}, u32[]{:S(2)}, u32[]{:S(2)}) collective-permute-start(bf16[1,2,2,2,32,256]{5,4,3,2,1,0:T(8,128)(2,1)S(1)} %get-tuple-element.9), channel_id=1, source_target_pairs={{0,2},{1,3},{2,0},{3,1},{4,6},{5,7},{6,4},{7,5},{8,10},{9,11},{10,... | collective-permute-start | bytes 393224 | tf_op jit(solution)/shard_map/ppermute | solution.py:138
  8.3 0.0 collective-permute-done.1
  8.3 2.7 %collective-permute-start.2 = (f32[2,56,128]{2,1,0:T(8,128)S(1)}, f32[2,56,128]{2,1,0:T(8,128)S(1)}, u32[]{:S(2)}, u32[]{:S(2)}) collective-permute-start(f32[2,56,128]{2,1,0:T(8,128)S(1)} %pad_maximum_fusion.4), channel_id=1, source_target_pairs={{0,9},{1,8},{2,11},{3,10},{4,13},{5,12},{6,15},{7,14},{8,1},{9,0},... | collective-permute-start | bytes 172040 | tf_op jit(solution)/shard_map/ppermute | solution.py:138
  11.1 1.5 %collective-permute-done.4 = bf16[1,2,2,2,32,256]{5,4,3,2,1,0:T(8,128)(2,1)S(1)} collective-permute-done((bf16[1,2,2,2,32,256]{5,4,3,2,1,0:T(8,128)(2,1)S(1)}, bf16[1,2,2,2,32,256]{5,4,3,2,1,0:T(8,128)(2,1)S(1)}, u32[]{:S(2)}, u32[]{:S(2)}) %collective-permute-start.4) | collective-permute-done | bytes 131104 | tf_op jit(solution)/shard_map/ppermute | solution.py:138
  12.6 0.3 %collective-permute-start.5 = (bf16[2,2,2,32,256]{4,3,2,1,0:T(8,128)(2,1)S(1)}, bf16[2,2,2,32,256]{4,3,2,1,0:T(8,128)(2,1)S(1)}, u32[]{:S(2)}, u32[]{:S(2)}) collective-permute-start(bf16[2,2,2,32,256]{4,3,2,1,0:T(8,128)(2,1)S(1)} %get-tuple-element.7), channel_id=1, source_target_pairs={{0,4},{1,5},{2,6},{3,7},{4,0},{5,1},{6,2},{7,3},{8,12},{9,13},{10,... | collective-permute-start | bytes 393224 | tf_op jit(solution)/shard_map/ppermute | solution.py:138
  12.9 0.2 collective-permute-done.2
  13.1 3.1 %collective-permute-start.3 = (f32[4,56,128]{2,1,0:T(8,128)S(1)}, f32[4,56,128]{2,1,0:T(8,128)S(1)}, u32[]{:S(2)}, u32[]{:S(2)}) collective-permute-start(f32[4,56,128]{2,1,0:T(8,128)S(1)} %pad_maximum_fusion.3), channel_id=1, source_target_pairs={{0,3},{1,2},{2,1},{3,0},{4,7},{5,6},{6,5},{7,4},{8,11},{9,10},{10,... | collective-permute-start | bytes 344072 | tf_op jit(solution)/shard_map/ppermute | solution.py:138
  16.2 1.5 %collective-permute-done.5 = bf16[2,2,2,32,256]{4,3,2,1,0:T(8,128)(2,1)S(1)} collective-permute-done((bf16[2,2,2,32,256]{4,3,2,1,0:T(8,128)(2,1)S(1)}, bf16[2,2,2,32,256]{4,3,2,1,0:T(8,128)(2,1)S(1)}, u32[]{:S(2)}, u32[]{:S(2)}) %collective-permute-start.5) | collective-permute-done | bytes 131104 | tf_op jit(solution)/shard_map/ppermute | solution.py:138
  17.7 0.1 collective-permute-start.6
  17.8 1.2 %collective-permute-done.3 = f32[4,56,128]{2,1,0:T(8,128)S(1)} collective-permute-done((f32[4,56,128]{2,1,0:T(8,128)S(1)}, f32[4,56,128]{2,1,0:T(8,128)S(1)}, u32[]{:S(2)}, u32[]{:S(2)}) %collective-permute-start.3) | collective-permute-done | bytes 114720 | tf_op jit(solution)/shard_map/ppermute | solution.py:138
  19.1 0.1 collective-permute-done.6
  19.2 0.7 %score_other.1 = f32[32,64]{1,0:T(8,128)S(1)} custom-call(f32[8,56,128]{2,1,0:T(8,128)S(1)} %pad_maximum_fusion.1.payload_ref, bf16[8,2,32,256]{3,2,1,0:T(8,128)(2,1)S(1)} %pad_maximum_fusion.query_ref), custom_call_target="tpu_custom_call" | custom-call | tf_op jit(solution)/shard_map/score_other/pallas_call | solution.py:121
  19.9 2.4 %collective-permute-start.7 = (f32[32,64]{1,0:T(8,128)S(1)}, f32[32,64]{1,0:T(8,128)S(1)}, u32[]{:S(2)}, u32[]{:S(2)}) collective-permute-start(f32[32,64]{1,0:T(8,128)S(1)} %score_other.1), channel_id=1, source_target_pairs={{0,9},{1,8},{2,11},{3,10},{4,13},{5,12},{6,15},{7,14},{8,1},{9,0},... | collective-permute-start | bytes 24584 | tf_op jit(solution)/shard_map/ppermute | solution.py:138
  22.2 0.7 %score_own.1 = f32[32,64]{1,0:T(8,128)S(1)} custom-call(f32[8,56,128]{2,1,0:T(8,128)S(1)} %pad_maximum_fusion.1.payload_ref, bf16[8,2,32,256]{3,2,1,0:T(8,128)(2,1)S(1)} %pad_maximum_fusion.query_ref), custom_call_target="tpu_custom_call" | custom-call | tf_op jit(solution)/shard_map/score_own/pallas_call | solution.py:121
  22.9 1.1 %collective-permute-done.7 = f32[32,64]{1,0:T(8,128)S(1)} collective-permute-done((f32[32,64]{1,0:T(8,128)S(1)}, f32[32,64]{1,0:T(8,128)S(1)}, u32[]{:S(2)}, u32[]{:S(2)}) %collective-permute-start.7) | collective-permute-done | bytes 8224 | tf_op jit(solution)/shard_map/ppermute | solution.py:138
  24.0 0.6 %add.67 = f32[32,64]{1,0:T(8,128)} add(f32[32,64]{1,0:T(8,128)S(1)} %score_own.1, f32[32,64]{1,0:T(8,128)S(1)} %collective-permute-done.7) | non-fusion elementwise | flops 2048 | bytes 24576 | tf_op jit(solution)/shard_map/add | solution.py:199
  (10 shorter events, 0.2 us)
Async XLA Ops:
  0.0 6.8 %copy-start = (bf16[512,256]{1,0:T(8,128)(2,1)S(1)}, bf16[512,256]{1,0:T(8,128)(2,1)}, u32[]{:S(2)}) copy-start(bf16[512,256]{1,0:T(8,128)(2,1)} %param.13) | copy-start | bytes 786436
  2.4 1.6 %collective-permute-start = (f32[56,128]{1,0:T(8,128)}, f32[56,128]{1,0:T(8,128)S(1)}, u32[]{:S(2)}, u32[]{:S(2)}) collective-permute-start(f32[56,128]{1,0:T(8,128)} %project.1), channel_id=1, source_target_pairs={{0,1},{1,0},{2,3},{3,2},{4,5},{5,4},{6,7},{7,6},{8,9},{9,8},{10,11... | collective-permute-start | bytes 86024 | tf_op jit(solution)/shard_map/ppermute | solution.py:138
  2.9 1.1 %copy-start.1 = (f32[56,128]{1,0:T(8,128)S(1)}, f32[56,128]{1,0:T(8,128)}, u32[]{:S(2)}) copy-start(f32[56,128]{1,0:T(8,128)} %project.1) | copy-start | bytes 86020
  4.0 4.3 %collective-permute-start.1 = (f32[1,56,128]{2,1,0:T(8,128)S(1)}, f32[1,56,128]{2,1,0:T(8,128)S(1)}, u32[]{:S(2)}, u32[]{:S(2)}) collective-permute-start(f32[1,56,128]{2,1,0:T(8,128)S(1)} %add_bitcast_fusion), channel_id=1, source_target_pairs={{0,5},{1,4},{2,7},{3,6},{4,1},{5,0},{6,3},{7,2},{8,13},{9,12},{10,... | collective-permute-start | bytes 86024 | tf_op jit(solution)/shard_map/ppermute | solution.py:138
  6.8 5.8 %collective-permute-start.4 = (bf16[1,2,2,2,32,256]{5,4,3,2,1,0:T(8,128)(2,1)S(1)}, bf16[1,2,2,2,32,256]{5,4,3,2,1,0:T(8,128)(2,1)S(1)}, u32[]{:S(2)}, u32[]{:S(2)}) collective-permute-start(bf16[1,2,2,2,32,256]{5,4,3,2,1,0:T(8,128)(2,1)S(1)} %get-tuple-element.9), channel_id=1, source_target_pairs={{0,2},{1,3},{2,0},{3,1},{4,6},{5,7},{6,4},{7,5},{8,10},{9,11},{10,... | collective-permute-start | bytes 393224 | tf_op jit(solution)/shard_map/ppermute | solution.py:138
  8.3 4.7 %collective-permute-start.2 = (f32[2,56,128]{2,1,0:T(8,128)S(1)}, f32[2,56,128]{2,1,0:T(8,128)S(1)}, u32[]{:S(2)}, u32[]{:S(2)}) collective-permute-start(f32[2,56,128]{2,1,0:T(8,128)S(1)} %pad_maximum_fusion.4), channel_id=1, source_target_pairs={{0,9},{1,8},{2,11},{3,10},{4,13},{5,12},{6,15},{7,14},{8,1},{9,0},... | collective-permute-start | bytes 172040 | tf_op jit(solution)/shard_map/ppermute | solution.py:138
  12.6 5.0 %collective-permute-start.5 = (bf16[2,2,2,32,256]{4,3,2,1,0:T(8,128)(2,1)S(1)}, bf16[2,2,2,32,256]{4,3,2,1,0:T(8,128)(2,1)S(1)}, u32[]{:S(2)}, u32[]{:S(2)}) collective-permute-start(bf16[2,2,2,32,256]{4,3,2,1,0:T(8,128)(2,1)S(1)} %get-tuple-element.7), channel_id=1, source_target_pairs={{0,4},{1,5},{2,6},{3,7},{4,0},{5,1},{6,2},{7,3},{8,12},{9,13},{10,... | collective-permute-start | bytes 393224 | tf_op jit(solution)/shard_map/ppermute | solution.py:138
  13.1 6.0 %collective-permute-start.3 = (f32[4,56,128]{2,1,0:T(8,128)S(1)}, f32[4,56,128]{2,1,0:T(8,128)S(1)}, u32[]{:S(2)}, u32[]{:S(2)}) collective-permute-start(f32[4,56,128]{2,1,0:T(8,128)S(1)} %pad_maximum_fusion.3), channel_id=1, source_target_pairs={{0,3},{1,2},{2,1},{3,0},{4,7},{5,6},{6,5},{7,4},{8,11},{9,10},{10,... | collective-permute-start | bytes 344072 | tf_op jit(solution)/shard_map/ppermute | solution.py:138
  17.7 1.4 %collective-permute-start.6 = (bf16[4,2,32,256]{3,2,1,0:T(8,128)(2,1)S(1)}, bf16[4,2,32,256]{3,2,1,0:T(8,128)(2,1)S(1)}, u32[]{:S(2)}, u32[]{:S(2)}) collective-permute-start(bf16[4,2,32,256]{3,2,1,0:T(8,128)(2,1)S(1)} %pad_maximum_fusion.2), channel_id=1, source_target_pairs={{0,1},{1,0},{2,3},{3,2},{4,5},{5,4},{6,7},{7,6},{8,9},{9,8},{10,11... | collective-permute-start | bytes 393224 | tf_op jit(solution)/shard_map/ppermute | solution.py:138
  19.9 4.1 %collective-permute-start.7 = (f32[32,64]{1,0:T(8,128)S(1)}, f32[32,64]{1,0:T(8,128)S(1)}, u32[]{:S(2)}, u32[]{:S(2)}) collective-permute-start(f32[32,64]{1,0:T(8,128)S(1)} %score_other.1), channel_id=1, source_target_pairs={{0,9},{1,8},{2,11},{3,10},{4,13},{5,12},{6,15},{7,14},{8,1},{9,0},... | collective-permute-start | bytes 24584 | tf_op jit(solution)/shard_map/ppermute | solution.py:138

commit v4 on v3

--- a/solution.py
+++ b/solution.py
@@ -63,7 +63,10 @@
     )(*operands)
 
 
-def score_kernel(row_count, rank, origins, other, payload_ref, query_ref, scores_ref, outward_ref):
+def score_kernel(row_count, rank, origins, other, *refs):
+    payload_ref, query_ref = refs[:2]
+    base_ref = refs[2] if len(refs) == 5 else None
+    scores_ref, outward_ref = refs[-2:]
     sources = payload_ref.shape[0]
     query_rows, columns = scores_ref.shape
     chunks, halves = query_ref.shape[:2]
@@ -107,14 +110,14 @@
 
     @pl.when(pl.program_id(0) == 0)
     def _():
-        scores_ref[...] = scores
+        scores_ref[...] = scores if base_ref is None else scores + base_ref[...]
 
     @pl.when(pl.program_id(0) > 0)
     def _():
         scores_ref[...] += scores
 
 
-def score(payload, query, columns, row_count, rank, origins, other):
+def score(payload, query, columns, row_count, rank, origins, other, base=None):
     sources = payload.shape[0]
     query_rows = query.shape[2]
     step = min(sources, 8)
@@ -124,13 +127,14 @@
         in_specs=[
             pl.BlockSpec((step,) + payload.shape[1:], lambda i: (i, 0, 0)),
             pl.BlockSpec(query.shape, lambda i: (0, 0, 0, 0)),
-        ],
+        ]
+        + [pl.BlockSpec((query_rows, columns), lambda i: (0, 0))] * (base is not None),
         out_specs=pl.BlockSpec((query_rows, columns), lambda i: (0, 0)),
         out_shape=jax.ShapeDtypeStruct((query_rows, columns), jnp.float32),
         scratch_shapes=[pltpu.VMEM((rank, step * row_count), jnp.float32)],
         compiler_params=pltpu.CompilerParams(vmem_limit_bytes=48 * 1024 * 1024),
         name="score_other" if other else "score_own",
-    )(payload, query)
+    )(payload, query, *([] if base is None else [base]))
 
 
 def exchange(value, axis, bit):
@@ -155,7 +159,7 @@
     here = lax.axis_index(both)
     half = here // (parts // 2)
     bits = [1 << place for place in range((parts // 2 - 1).bit_length())]
-    order = [bit for bit in bits if bit >= cut_count] + [bit for bit in bits if bit < cut_count]
+    order = bits
     waiting = bits[::-1]
     arrived = queries.reshape([1, 2] + [2] * len(bits) + [query_rows, width])
     origins = [0]
@@ -191,11 +195,16 @@
         bit *= 2
     payload = payload[None]
     far = [bit for bit in bits + [parts // 2] if bit >= cut_count]
-    for bit in far[-2:] + far[-3::-1]:
+    *early, last = far[-2:] + far[-3::-1]
+    for bit in early:
         payload = jnp.concatenate([payload, exchange(payload, both, bit ^ flip)], axis=0)
+    landed = exchange(payload, both, last ^ flip)
     columns = doc_slots.shape[0]
-    theirs = score(payload, arrived, columns, row_count, rank, origins, True)
-    own = score(payload, arrived, columns, row_count, rank, origins, False)
+    sizes = (columns, row_count, rank, origins)
+    theirs = score(payload, arrived, *sizes, True)
+    theirs = score(landed, arrived, *sizes, True, theirs)
+    own = score(payload, arrived, *sizes, False)
+    own = score(landed, arrived, *sizes, False, own)
     return own + exchange(theirs, both, parts // 2 ^ flip)
 
 

time: 24.7 us -> 24.6 us (level)
  Pallas kernels: 3.73 us -> 4.39 us
  waiting for transfers between devices: 6.64 us -> 5.98 us
    pallas_call x2 -> x4, Pallas kernels: 1.32 us -> 1.99 us  [score(): pl.pallas_call(functools.partial(score_kernel, row_count, rank, origins,...]
    ppermute x8, waiting for transfers between devices: 6.64 us -> 5.98 us  [exchange(): return lax.ppermute(value, axis, [(i, i ^ bit) for i in range(count)])]
  transfers between devices with their start and end apart: 8 -> 8, of which waited for: 7 -> 5; matrix products, arithmetic and copies ran while one was open for 1% -> 1% of each run, Pallas kernels for 3% -> 6%
where the time goes in v4:
time: 24.6 us; the launch traced here: 24.5 us
  starting transfers between devices  13.2 us (54%)
  waiting for transfers between devices  5.98 us (24%)
  Pallas kernels  4.39 us (18%)
  other arithmetic  0.72 us (3%)
    ppermute x8, starting transfers between devices, exchange(): return lax.ppermute(value, axis, [(i, i ^ bit) for i in range(count)])  13.2 us
    ppermute x8, waiting for transfers between devices, exchange(): return lax.ppermute(value, axis, [(i, i ^ bit) for i in range(count)])  5.98 us
    pallas_call x1, Pallas kernels, project(): pl.pallas_call(project_kernel, in_specs=[pl.BlockSpec(memory_space=pltpu....  2.4 us
    pallas_call x4, Pallas kernels, score(): pl.pallas_call(functools.partial(score_kernel, row_count, rank, origins,...  1.99 us
    add x1, other arithmetic, on_device(): return own + exchange(theirs, both, parts // 2 ^ flip)  0.61 us
  transfers between devices with their start and end apart: 8, of which 5 were waited for; matrix products, arithmetic and copies ran while one was open for 1% of the time, Pallas kernels for 6%

profile of v4, /device:TPU:0, one launch (start us, length us, event | category | flops | bytes accessed | tf_op | source)
XLA Modules:
  0.0 24.5 jit_solution(6824984167569256146)
XLA Ops:
  0.0 2.4 %project.1 = f32[56,128]{1,0:T(8,128)} custom-call(bf16[48,3584]{1,0:T(8,128)(2,1)} %refs_0_.1, bf16[64,3584]{1,0:T(8,128)(2,1)} %bitcast.21, bf16[48,2048]{1,0:T(8,128)(2,1)} %refs_2_.1, bf16[64,2048]{1,0:T(8,128)(2,1)} %bitcast.23, s32[1,8]{1,0:T(1,128)} %refs_4_.1, s32[64]{0:T(128)} %refs_5_.1), custom_call_target="tpu_custom_call" | custom-call | tf_op jit(solution)/shard_map/project/pallas_call | solution.py:54
  2.4 0.5 %collective-permute-start = (f32[56,128]{1,0:T(8,128)}, f32[56,128]{1,0:T(8,128)S(1)}, u32[]{:S(2)}, u32[]{:S(2)}) collective-permute-start(f32[56,128]{1,0:T(8,128)} %project.1), channel_id=1, source_target_pairs={{0,1},{1,0},{2,3},{3,2},{4,5},{5,4},{6,7},{7,6},{8,9},{9,8},{10,11... | collective-permute-start | bytes 86024 | tf_op jit(solution)/shard_map/ppermute | solution.py:142
  2.9 0.0 copy-done
  3.0 0.0 copy-start.1
  3.0 0.1 collective-permute-start.4
  3.2 0.8 %collective-permute-done = f32[56,128]{1,0:T(8,128)S(1)} collective-permute-done((f32[56,128]{1,0:T(8,128)}, f32[56,128]{1,0:T(8,128)S(1)}, u32[]{:S(2)}, u32[]{:S(2)}) %collective-permute-start) | collective-permute-done | bytes 28704 | tf_op jit(solution)/shard_map/ppermute | solution.py:142
  4.0 2.7 %collective-permute-start.1 = (f32[1,56,128]{2,1,0:T(8,128)S(1)}, f32[1,56,128]{2,1,0:T(8,128)S(1)}, u32[]{:S(2)}, u32[]{:S(2)}) collective-permute-start(f32[1,56,128]{2,1,0:T(8,128)S(1)} %add_bitcast_fusion), channel_id=1, source_target_pairs={{0,5},{1,4},{2,7},{3,6},{4,1},{5,0},{6,3},{7,2},{8,13},{9,12},{10,... | collective-permute-start | bytes 86024 | tf_op jit(solution)/shard_map/ppermute | solution.py:142
  6.7 0.0 collective-permute-done.4
  6.8 1.6 %collective-permute-start.5 = (bf16[2,2,2,32,256]{4,3,2,1,0:T(8,128)(2,1)S(1)}, bf16[2,2,2,32,256]{4,3,2,1,0:T(8,128)(2,1)S(1)}, u32[]{:S(2)}, u32[]{:S(2)}) collective-permute-start(bf16[2,2,2,32,256]{4,3,2,1,0:T(8,128)(2,1)S(1)} %get-tuple-element.7), channel_id=1, source_target_pairs={{0,2},{1,3},{2,0},{3,1},{4,6},{5,7},{6,4},{7,5},{8,10},{9,11},{10,... | collective-permute-start | bytes 393224 | tf_op jit(solution)/shard_map/ppermute | solution.py:142
  8.4 0.0 collective-permute-done.1
  8.4 2.7 %collective-permute-start.2 = (f32[2,56,128]{2,1,0:T(8,128)S(1)}, f32[2,56,128]{2,1,0:T(8,128)S(1)}, u32[]{:S(2)}, u32[]{:S(2)}) collective-permute-start(f32[2,56,128]{2,1,0:T(8,128)S(1)} %pad_maximum_fusion.4), channel_id=1, source_target_pairs={{0,9},{1,8},{2,11},{3,10},{4,13},{5,12},{6,15},{7,14},{8,1},{9,0},... | collective-permute-start | bytes 172040 | tf_op jit(solution)/shard_map/ppermute | solution.py:142
  11.1 1.6 %collective-permute-done.5 = bf16[2,2,2,32,256]{4,3,2,1,0:T(8,128)(2,1)S(1)} collective-permute-done((bf16[2,2,2,32,256]{4,3,2,1,0:T(8,128)(2,1)S(1)}, bf16[2,2,2,32,256]{4,3,2,1,0:T(8,128)(2,1)S(1)}, u32[]{:S(2)}, u32[]{:S(2)}) %collective-permute-start.5) | collective-permute-done | bytes 131104 | tf_op jit(solution)/shard_map/ppermute | solution.py:142
  12.7 0.5 %collective-permute-start.6 = (bf16[4,2,32,256]{3,2,1,0:T(8,128)(2,1)S(1)}, bf16[4,2,32,256]{3,2,1,0:T(8,128)(2,1)S(1)}, u32[]{:S(2)}, u32[]{:S(2)}) collective-permute-start(bf16[4,2,32,256]{3,2,1,0:T(8,128)(2,1)S(1)} %get-tuple-element.6), channel_id=1, source_target_pairs={{0,4},{1,5},{2,6},{3,7},{4,0},{5,1},{6,2},{7,3},{8,12},{9,13},{10,... | collective-permute-start | bytes 393224 | tf_op jit(solution)/shard_map/ppermute | solution.py:142
  13.2 0.0 collective-permute-done.2
  13.2 3.0 %collective-permute-start.3 = (f32[4,56,128]{2,1,0:T(8,128)S(1)}, f32[4,56,128]{2,1,0:T(8,128)S(1)}, u32[]{:S(2)}, u32[]{:S(2)}) collective-permute-start(f32[4,56,128]{2,1,0:T(8,128)S(1)} %pad_maximum_fusion.3.refs_0_), channel_id=1, source_target_pairs={{0,3},{1,2},{2,1},{3,0},{4,7},{5,6},{6,5},{7,4},{8,11},{9,10},{10,... | collective-permute-start | bytes 344072 | tf_op jit(solution)/shard_map/ppermute | solution.py:142
  16.2 1.5 %collective-permute-done.6 = bf16[4,2,32,256]{3,2,1,0:T(8,128)(2,1)S(1)} collective-permute-done((bf16[4,2,32,256]{3,2,1,0:T(8,128)(2,1)S(1)}, bf16[4,2,32,256]{3,2,1,0:T(8,128)(2,1)S(1)}, u32[]{:S(2)}, u32[]{:S(2)}) %collective-permute-start.6) | collective-permute-done | bytes 131104 | tf_op jit(solution)/shard_map/ppermute | solution.py:142
  17.7 0.5 %score_other.2.refs_2_ = f32[32,64]{1,0:T(8,128)S(1)} custom-call(f32[4,56,128]{2,1,0:T(8,128)S(1)} %pad_maximum_fusion.3.refs_0_, bf16[8,2,32,256]{3,2,1,0:T(8,128)(2,1)S(1)} %pad_maximum_fusion.1.refs_1_), custom_call_target="tpu_custom_call" | custom-call | tf_op jit(solution)/shard_map/score_other/pallas_call | solution.py:124
  18.2 0.9 %collective-permute-done.3.refs_0_ = f32[4,56,128]{2,1,0:T(8,128)S(1)} collective-permute-done((f32[4,56,128]{2,1,0:T(8,128)S(1)}, f32[4,56,128]{2,1,0:T(8,128)S(1)}, u32[]{:S(2)}, u32[]{:S(2)}) %collective-permute-start.3) | collective-permute-done | bytes 114720 | tf_op jit(solution)/shard_map/ppermute | solution.py:142
  19.1 0.5 %score_other.3 = f32[32,64]{1,0:T(8,128)S(1)} custom-call(f32[4,56,128]{2,1,0:T(8,128)S(1)} %collective-permute-done.3.refs_0_, bf16[8,2,32,256]{3,2,1,0:T(8,128)(2,1)S(1)} %pad_maximum_fusion.1.refs_1_, f32[32,64]{1,0:T(8,128)S(1)} %score_other.2.refs_2_), custom_call_target="tpu_custom_call" | custom-call | tf_op jit(solution)/shard_map/score_other/pallas_call | solution.py:124
  19.6 2.1 %collective-permute-start.7 = (f32[32,64]{1,0:T(8,128)S(1)}, f32[32,64]{1,0:T(8,128)S(1)}, u32[]{:S(2)}, u32[]{:S(2)}) collective-permute-start(f32[32,64]{1,0:T(8,128)S(1)} %score_other.3), channel_id=1, source_target_pairs={{0,9},{1,8},{2,11},{3,10},{4,13},{5,12},{6,15},{7,14},{8,1},{9,0},... | collective-permute-start | bytes 24584 | tf_op jit(solution)/shard_map/ppermute | solution.py:142
  21.7 0.5 %score_own.2.refs_2_ = f32[32,64]{1,0:T(8,128)S(1)} custom-call(f32[4,56,128]{2,1,0:T(8,128)S(1)} %pad_maximum_fusion.3.refs_0_, bf16[8,2,32,256]{3,2,1,0:T(8,128)(2,1)S(1)} %pad_maximum_fusion.1.refs_1_), custom_call_target="tpu_custom_call" | custom-call | tf_op jit(solution)/shard_map/score_own/pallas_call | solution.py:124
  22.2 0.5 %score_own.3 = f32[32,64]{1,0:T(8,128)S(1)} custom-call(f32[4,56,128]{2,1,0:T(8,128)S(1)} %collective-permute-done.3.refs_0_, bf16[8,2,32,256]{3,2,1,0:T(8,128)(2,1)S(1)} %pad_maximum_fusion.1.refs_1_, f32[32,64]{1,0:T(8,128)S(1)} %score_own.2.refs_2_), custom_call_target="tpu_custom_call" | custom-call | tf_op jit(solution)/shard_map/score_own/pallas_call | solution.py:124
  22.7 1.2 %collective-permute-done.7 = f32[32,64]{1,0:T(8,128)S(1)} collective-permute-done((f32[32,64]{1,0:T(8,128)S(1)}, f32[32,64]{1,0:T(8,128)S(1)}, u32[]{:S(2)}, u32[]{:S(2)}) %collective-permute-start.7) | collective-permute-done | bytes 8224 | tf_op jit(solution)/shard_map/ppermute | solution.py:142
  23.9 0.6 %add.67 = f32[32,64]{1,0:T(8,128)} add(f32[32,64]{1,0:T(8,128)S(1)} %score_own.3, f32[32,64]{1,0:T(8,128)S(1)} %collective-permute-done.7) | non-fusion elementwise | flops 2048 | bytes 24576 | tf_op jit(solution)/shard_map/add | solution.py:208
  (12 shorter events, 0.2 us)
Async XLA Ops:
  0.0 2.9 %copy-start = (bf16[512,256]{1,0:T(8,128)(2,1)S(1)}, bf16[512,256]{1,0:T(8,128)(2,1)}, u32[]{:S(2)}) copy-start(bf16[512,256]{1,0:T(8,128)(2,1)} %param.13) | copy-start | bytes 786436
  2.4 1.6 %collective-permute-start = (f32[56,128]{1,0:T(8,128)}, f32[56,128]{1,0:T(8,128)S(1)}, u32[]{:S(2)}, u32[]{:S(2)}) collective-permute-start(f32[56,128]{1,0:T(8,128)} %project.1), channel_id=1, source_target_pairs={{0,1},{1,0},{2,3},{3,2},{4,5},{5,4},{6,7},{7,6},{8,9},{9,8},{10,11... | collective-permute-start | bytes 86024 | tf_op jit(solution)/shard_map/ppermute | solution.py:142
  3.0 1.0 %copy-start.1 = (f32[56,128]{1,0:T(8,128)S(1)}, f32[56,128]{1,0:T(8,128)}, u32[]{:S(2)}) copy-start(f32[56,128]{1,0:T(8,128)} %project.1) | copy-start | bytes 86020
  3.0 3.7 %collective-permute-start.4 = (bf16[1,2,2,2,32,256]{5,4,3,2,1,0:T(8,128)(2,1)S(1)}, bf16[1,2,2,2,32,256]{5,4,3,2,1,0:T(8,128)(2,1)S(1)}, u32[]{:S(2)}, u32[]{:S(2)}) collective-permute-start(bf16[1,2,2,2,32,256]{5,4,3,2,1,0:T(8,128)(2,1)S(1)} %pad_maximum_fusion.2), channel_id=1, source_target_pairs={{0,1},{1,0},{2,3},{3,2},{4,5},{5,4},{6,7},{7,6},{8,9},{9,8},{10,11... | collective-permute-start | bytes 393224 | tf_op jit(solution)/shard_map/ppermute | solution.py:142
  4.0 4.4 %collective-permute-start.1 = (f32[1,56,128]{2,1,0:T(8,128)S(1)}, f32[1,56,128]{2,1,0:T(8,128)S(1)}, u32[]{:S(2)}, u32[]{:S(2)}) collective-permute-start(f32[1,56,128]{2,1,0:T(8,128)S(1)} %add_bitcast_fusion), channel_id=1, source_target_pairs={{0,5},{1,4},{2,7},{3,6},{4,1},{5,0},{6,3},{7,2},{8,13},{9,12},{10,... | collective-permute-start | bytes 86024 | tf_op jit(solution)/shard_map/ppermute | solution.py:142
  6.8 5.8 %collective-permute-start.5 = (bf16[2,2,2,32,256]{4,3,2,1,0:T(8,128)(2,1)S(1)}, bf16[2,2,2,32,256]{4,3,2,1,0:T(8,128)(2,1)S(1)}, u32[]{:S(2)}, u32[]{:S(2)}) collective-permute-start(bf16[2,2,2,32,256]{4,3,2,1,0:T(8,128)(2,1)S(1)} %get-tuple-element.7), channel_id=1, source_target_pairs={{0,2},{1,3},{2,0},{3,1},{4,6},{5,7},{6,4},{7,5},{8,10},{9,11},{10,... | collective-permute-start | bytes 393224 | tf_op jit(solution)/shard_map/ppermute | solution.py:142
  8.4 4.8 %collective-permute-start.2 = (f32[2,56,128]{2,1,0:T(8,128)S(1)}, f32[2,56,128]{2,1,0:T(8,128)S(1)}, u32[]{:S(2)}, u32[]{:S(2)}) collective-permute-start(f32[2,56,128]{2,1,0:T(8,128)S(1)} %pad_maximum_fusion.4), channel_id=1, source_target_pairs={{0,9},{1,8},{2,11},{3,10},{4,13},{5,12},{6,15},{7,14},{8,1},{9,0},... | collective-permute-start | bytes 172040 | tf_op jit(solution)/shard_map/ppermute | solution.py:142
  12.7 5.0 %collective-permute-start.6 = (bf16[4,2,32,256]{3,2,1,0:T(8,128)(2,1)S(1)}, bf16[4,2,32,256]{3,2,1,0:T(8,128)(2,1)S(1)}, u32[]{:S(2)}, u32[]{:S(2)}) collective-permute-start(bf16[4,2,32,256]{3,2,1,0:T(8,128)(2,1)S(1)} %get-tuple-element.6), channel_id=1, source_target_pairs={{0,4},{1,5},{2,6},{3,7},{4,0},{5,1},{6,2},{7,3},{8,12},{9,13},{10,... | collective-permute-start | bytes 393224 | tf_op jit(solution)/shard_map/ppermute | solution.py:142
  13.2 5.9 %collective-permute-start.3 = (f32[4,56,128]{2,1,0:T(8,128)S(1)}, f32[4,56,128]{2,1,0:T(8,128)S(1)}, u32[]{:S(2)}, u32[]{:S(2)}) collective-permute-start(f32[4,56,128]{2,1,0:T(8,128)S(1)} %pad_maximum_fusion.3.refs_0_), channel_id=1, source_target_pairs={{0,3},{1,2},{2,1},{3,0},{4,7},{5,6},{6,5},{7,4},{8,11},{9,10},{10,... | collective-permute-start | bytes 344072 | tf_op jit(solution)/shard_map/ppermute | solution.py:142
  19.6 4.3 %collective-permute-start.7 = (f32[32,64]{1,0:T(8,128)S(1)}, f32[32,64]{1,0:T(8,128)S(1)}, u32[]{:S(2)}, u32[]{:S(2)}) collective-permute-start(f32[32,64]{1,0:T(8,128)S(1)} %score_other.3), channel_id=1, source_target_pairs={{0,9},{1,8},{2,11},{3,10},{4,13},{5,12},{6,15},{7,14},{8,1},{9,0},... | collective-permute-start | bytes 24584 | tf_op jit(solution)/shard_map/ppermute | solution.py:142

commit v5 on v4

--- a/solution.py
+++ b/solution.py
@@ -198,7 +198,7 @@
     *early, last = far[-2:] + far[-3::-1]
     for bit in early:
         payload = jnp.concatenate([payload, exchange(payload, both, bit ^ flip)], axis=0)
-    landed = exchange(payload, both, last ^ flip)
+    landed = exchange(payload, both, last)
     columns = doc_slots.shape[0]
     sizes = (columns, row_count, rank, origins)
     theirs = score(payload, arrived, *sizes, True)

time: 24.6 us -> 24.4 us (level); the launches traced: 24.5 us -> 24 us
  starting transfers between devices: 13.2 us -> 11.8 us
  waiting for transfers between devices: 5.98 us -> 6.93 us
    ppermute x8, starting transfers between devices: 13.2 us -> 11.8 us  [exchange(): return lax.ppermute(value, axis, [(i, i ^ bit) for i in range(count)])]
    ppermute x8, waiting for transfers between devices: 5.98 us -> 6.93 us  [exchange(): return lax.ppermute(value, axis, [(i, i ^ bit) for i in range(count)])]
where the time goes in v5:
time: 24.4 us; the launch traced here: 24 us
  starting transfers between devices  11.8 us (48%)
  waiting for transfers between devices  6.93 us (28%)
  Pallas kernels  4.39 us (18%)
  other arithmetic  0.72 us (3%)
    ppermute x8, starting transfers between devices, exchange(): return lax.ppermute(value, axis, [(i, i ^ bit) for i in range(count)])  11.8 us
    ppermute x8, waiting for transfers between devices, exchange(): return lax.ppermute(value, axis, [(i, i ^ bit) for i in range(count)])  6.93 us
    pallas_call x1, Pallas kernels, project(): pl.pallas_call(project_kernel, in_specs=[pl.BlockSpec(memory_space=pltpu....  2.4 us
    pallas_call x4, Pallas kernels, score(): pl.pallas_call(functools.partial(score_kernel, row_count, rank, origins,...  1.99 us
    add x1, other arithmetic, on_device(): return own + exchange(theirs, both, parts // 2 ^ flip)  0.61 us
  transfers between devices with their start and end apart: 8, of which 5 were waited for; matrix products, arithmetic and copies ran while one was open for 1% of the time, Pallas kernels for 6%

profile of v5, /device:TPU:0, one launch (start us, length us, event | category | flops | bytes accessed | tf_op | source)
XLA Modules:
  0.0 24.0 jit_solution(270209885872324555)
XLA Ops:
  0.0 2.4 %project.1 = f32[56,128]{1,0:T(8,128)} custom-call(bf16[48,3584]{1,0:T(8,128)(2,1)} %refs_0_.1, bf16[64,3584]{1,0:T(8,128)(2,1)} %bitcast.21, bf16[48,2048]{1,0:T(8,128)(2,1)} %refs_2_.1, bf16[64,2048]{1,0:T(8,128)(2,1)} %bitcast.23, s32[1,8]{1,0:T(1,128)} %refs_4_.1, s32[64]{0:T(128)} %refs_5_.1), custom_call_target="tpu_custom_call" | custom-call | tf_op jit(solution)/shard_map/project/pallas_call | solution.py:54
  2.4 0.5 %collective-permute-start = (f32[56,128]{1,0:T(8,128)}, f32[56,128]{1,0:T(8,128)S(1)}, u32[]{:S(2)}, u32[]{:S(2)}) collective-permute-start(f32[56,128]{1,0:T(8,128)} %project.1), channel_id=1, source_target_pairs={{0,1},{1,0},{2,3},{3,2},{4,5},{5,4},{6,7},{7,6},{8,9},{9,8},{10,11... | collective-permute-start | bytes 86024 | tf_op jit(solution)/shard_map/ppermute | solution.py:142
  2.9 0.0 copy-done
  3.0 0.1 collective-permute-start.4
  3.2 0.8 %collective-permute-done = f32[56,128]{1,0:T(8,128)S(1)} collective-permute-done((f32[56,128]{1,0:T(8,128)}, f32[56,128]{1,0:T(8,128)S(1)}, u32[]{:S(2)}, u32[]{:S(2)}) %collective-permute-start) | collective-permute-done | bytes 28704 | tf_op jit(solution)/shard_map/ppermute | solution.py:142
  4.0 0.0 copy-done.1
  4.0 2.7 %collective-permute-start.1 = (f32[1,56,128]{2,1,0:T(8,128)S(1)}, f32[1,56,128]{2,1,0:T(8,128)S(1)}, u32[]{:S(2)}, u32[]{:S(2)}) collective-permute-start(f32[1,56,128]{2,1,0:T(8,128)S(1)} %add_bitcast_fusion), channel_id=1, source_target_pairs={{0,5},{1,4},{2,7},{3,6},{4,1},{5,0},{6,3},{7,2},{8,13},{9,12},{10,... | collective-permute-start | bytes 86024 | tf_op jit(solution)/shard_map/ppermute | solution.py:142
  6.7 0.0 collective-permute-done.4
  6.8 1.6 %collective-permute-start.5 = (bf16[2,2,2,32,256]{4,3,2,1,0:T(8,128)(2,1)S(1)}, bf16[2,2,2,32,256]{4,3,2,1,0:T(8,128)(2,1)S(1)}, u32[]{:S(2)}, u32[]{:S(2)}) collective-permute-start(bf16[2,2,2,32,256]{4,3,2,1,0:T(8,128)(2,1)S(1)} %get-tuple-element.7), channel_id=1, source_target_pairs={{0,2},{1,3},{2,0},{3,1},{4,6},{5,7},{6,4},{7,5},{8,10},{9,11},{10,... | collective-permute-start | bytes 393224 | tf_op jit(solution)/shard_map/ppermute | solution.py:142
  8.4 0.0 collective-permute-done.1
  8.4 2.7 %collective-permute-start.2 = (f32[2,56,128]{2,1,0:T(8,128)S(1)}, f32[2,56,128]{2,1,0:T(8,128)S(1)}, u32[]{:S(2)}, u32[]{:S(2)}) collective-permute-start(f32[2,56,128]{2,1,0:T(8,128)S(1)} %pad_maximum_fusion.4), channel_id=1, source_target_pairs={{0,9},{1,8},{2,11},{3,10},{4,13},{5,12},{6,15},{7,14},{8,1},{9,0},... | collective-permute-start | bytes 172040 | tf_op jit(solution)/shard_map/ppermute | solution.py:142
  11.1 1.6 %collective-permute-done.5 = bf16[2,2,2,32,256]{4,3,2,1,0:T(8,128)(2,1)S(1)} collective-permute-done((bf16[2,2,2,32,256]{4,3,2,1,0:T(8,128)(2,1)S(1)}, bf16[2,2,2,32,256]{4,3,2,1,0:T(8,128)(2,1)S(1)}, u32[]{:S(2)}, u32[]{:S(2)}) %collective-permute-start.5) | collective-permute-done | bytes 131104 | tf_op jit(solution)/shard_map/ppermute | solution.py:142
  12.7 0.5 %collective-permute-start.6 = (bf16[4,2,32,256]{3,2,1,0:T(8,128)(2,1)S(1)}, bf16[4,2,32,256]{3,2,1,0:T(8,128)(2,1)S(1)}, u32[]{:S(2)}, u32[]{:S(2)}) collective-permute-start(bf16[4,2,32,256]{3,2,1,0:T(8,128)(2,1)S(1)} %get-tuple-element.6), channel_id=1, source_target_pairs={{0,4},{1,5},{2,6},{3,7},{4,0},{5,1},{6,2},{7,3},{8,12},{9,13},{10,... | collective-permute-start | bytes 393224 | tf_op jit(solution)/shard_map/ppermute | solution.py:142
  13.2 0.0 collective-permute-done.2
  13.2 1.9 %collective-permute-start.3 = (f32[4,56,128]{2,1,0:T(8,128)S(1)}, f32[4,56,128]{2,1,0:T(8,128)S(1)}, u32[]{:S(2)}, u32[]{:S(2)}) collective-permute-start(f32[4,56,128]{2,1,0:T(8,128)S(1)} %pad_maximum_fusion.3.refs_0_), channel_id=1, source_target_pairs={{0,2},{1,3},{2,0},{3,1},{4,6},{5,7},{6,4},{7,5},{8,10},{9,11},{10,... | collective-permute-start | bytes 344072 | tf_op jit(solution)/shard_map/ppermute | solution.py:142
  15.1 2.6 %collective-permute-done.6 = bf16[4,2,32,256]{3,2,1,0:T(8,128)(2,1)S(1)} collective-permute-done((bf16[4,2,32,256]{3,2,1,0:T(8,128)(2,1)S(1)}, bf16[4,2,32,256]{3,2,1,0:T(8,128)(2,1)S(1)}, u32[]{:S(2)}, u32[]{:S(2)}) %collective-permute-start.6) | collective-permute-done | bytes 131104 | tf_op jit(solution)/shard_map/ppermute | solution.py:142
  17.7 0.5 %score_other.2.refs_2_ = f32[32,64]{1,0:T(8,128)S(1)} custom-call(f32[4,56,128]{2,1,0:T(8,128)S(1)} %pad_maximum_fusion.3.refs_0_, bf16[8,2,32,256]{3,2,1,0:T(8,128)(2,1)S(1)} %pad_maximum_fusion.1.refs_1_), custom_call_target="tpu_custom_call" | custom-call | tf_op jit(solution)/shard_map/score_other/pallas_call | solution.py:124
  18.2 0.5 %collective-permute-done.3.refs_0_ = f32[4,56,128]{2,1,0:T(8,128)S(1)} collective-permute-done((f32[4,56,128]{2,1,0:T(8,128)S(1)}, f32[4,56,128]{2,1,0:T(8,128)S(1)}, u32[]{:S(2)}, u32[]{:S(2)}) %collective-permute-start.3) | collective-permute-done | bytes 114720 | tf_op jit(solution)/shard_map/ppermute | solution.py:142
  18.7 0.5 %score_other.3 = f32[32,64]{1,0:T(8,128)S(1)} custom-call(f32[4,56,128]{2,1,0:T(8,128)S(1)} %collective-permute-done.3.refs_0_, bf16[8,2,32,256]{3,2,1,0:T(8,128)(2,1)S(1)} %pad_maximum_fusion.1.refs_1_, f32[32,64]{1,0:T(8,128)S(1)} %score_other.2.refs_2_), custom_call_target="tpu_custom_call" | custom-call | tf_op jit(solution)/shard_map/score_other/pallas_call | solution.py:124
  19.2 1.8 %collective-permute-start.7 = (f32[32,64]{1,0:T(8,128)S(1)}, f32[32,64]{1,0:T(8,128)S(1)}, u32[]{:S(2)}, u32[]{:S(2)}) collective-permute-start(f32[32,64]{1,0:T(8,128)S(1)} %score_other.3), channel_id=1, source_target_pairs={{0,9},{1,8},{2,11},{3,10},{4,13},{5,12},{6,15},{7,14},{8,1},{9,0},... | collective-permute-start | bytes 24584 | tf_op jit(solution)/shard_map/ppermute | solution.py:142
  21.0 0.5 %score_own.2.refs_2_ = f32[32,64]{1,0:T(8,128)S(1)} custom-call(f32[4,56,128]{2,1,0:T(8,128)S(1)} %pad_maximum_fusion.3.refs_0_, bf16[8,2,32,256]{3,2,1,0:T(8,128)(2,1)S(1)} %pad_maximum_fusion.1.refs_1_), custom_call_target="tpu_custom_call" | custom-call | tf_op jit(solution)/shard_map/score_own/pallas_call | solution.py:124
  21.5 0.5 %score_own.3 = f32[32,64]{1,0:T(8,128)S(1)} custom-call(f32[4,56,128]{2,1,0:T(8,128)S(1)} %collective-permute-done.3.refs_0_, bf16[8,2,32,256]{3,2,1,0:T(8,128)(2,1)S(1)} %pad_maximum_fusion.1.refs_1_, f32[32,64]{1,0:T(8,128)S(1)} %score_own.2.refs_2_), custom_call_target="tpu_custom_call" | custom-call | tf_op jit(solution)/shard_map/score_own/pallas_call | solution.py:124
  22.0 1.4 %collective-permute-done.7 = f32[32,64]{1,0:T(8,128)S(1)} collective-permute-done((f32[32,64]{1,0:T(8,128)S(1)}, f32[32,64]{1,0:T(8,128)S(1)}, u32[]{:S(2)}, u32[]{:S(2)}) %collective-permute-start.7) | collective-permute-done | bytes 8224 | tf_op jit(solution)/shard_map/ppermute | solution.py:142
  23.4 0.6 %add.67 = f32[32,64]{1,0:T(8,128)} add(f32[32,64]{1,0:T(8,128)S(1)} %score_own.3, f32[32,64]{1,0:T(8,128)S(1)} %collective-permute-done.7) | non-fusion elementwise | flops 2048 | bytes 24576 | tf_op jit(solution)/shard_map/add | solution.py:208
  (12 shorter events, 0.2 us)
Async XLA Ops:
  0.0 2.9 %copy-start = (bf16[512,256]{1,0:T(8,128)(2,1)S(1)}, bf16[512,256]{1,0:T(8,128)(2,1)}, u32[]{:S(2)}) copy-start(bf16[512,256]{1,0:T(8,128)(2,1)} %param.13) | copy-start | bytes 786436
  2.4 1.6 %collective-permute-start = (f32[56,128]{1,0:T(8,128)}, f32[56,128]{1,0:T(8,128)S(1)}, u32[]{:S(2)}, u32[]{:S(2)}) collective-permute-start(f32[56,128]{1,0:T(8,128)} %project.1), channel_id=1, source_target_pairs={{0,1},{1,0},{2,3},{3,2},{4,5},{5,4},{6,7},{7,6},{8,9},{9,8},{10,11... | collective-permute-start | bytes 86024 | tf_op jit(solution)/shard_map/ppermute | solution.py:142
  3.0 1.0 %copy-start.1 = (f32[56,128]{1,0:T(8,128)S(1)}, f32[56,128]{1,0:T(8,128)}, u32[]{:S(2)}) copy-start(f32[56,128]{1,0:T(8,128)} %project.1) | copy-start | bytes 86020
  3.0 3.7 %collective-permute-start.4 = (bf16[1,2,2,2,32,256]{5,4,3,2,1,0:T(8,128)(2,1)S(1)}, bf16[1,2,2,2,32,256]{5,4,3,2,1,0:T(8,128)(2,1)S(1)}, u32[]{:S(2)}, u32[]{:S(2)}) collective-permute-start(bf16[1,2,2,2,32,256]{5,4,3,2,1,0:T(8,128)(2,1)S(1)} %pad_maximum_fusion.2), channel_id=1, source_target_pairs={{0,1},{1,0},{2,3},{3,2},{4,5},{5,4},{6,7},{7,6},{8,9},{9,8},{10,11... | collective-permute-start | bytes 393224 | tf_op jit(solution)/shard_map/ppermute | solution.py:142
  4.0 4.4 %collective-permute-start.1 = (f32[1,56,128]{2,1,0:T(8,128)S(1)}, f32[1,56,128]{2,1,0:T(8,128)S(1)}, u32[]{:S(2)}, u32[]{:S(2)}) collective-permute-start(f32[1,56,128]{2,1,0:T(8,128)S(1)} %add_bitcast_fusion), channel_id=1, source_target_pairs={{0,5},{1,4},{2,7},{3,6},{4,1},{5,0},{6,3},{7,2},{8,13},{9,12},{10,... | collective-permute-start | bytes 86024 | tf_op jit(solution)/shard_map/ppermute | solution.py:142
  6.8 5.8 %collective-permute-start.5 = (bf16[2,2,2,32,256]{4,3,2,1,0:T(8,128)(2,1)S(1)}, bf16[2,2,2,32,256]{4,3,2,1,0:T(8,128)(2,1)S(1)}, u32[]{:S(2)}, u32[]{:S(2)}) collective-permute-start(bf16[2,2,2,32,256]{4,3,2,1,0:T(8,128)(2,1)S(1)} %get-tuple-element.7), channel_id=1, source_target_pairs={{0,2},{1,3},{2,0},{3,1},{4,6},{5,7},{6,4},{7,5},{8,10},{9,11},{10,... | collective-permute-start | bytes 393224 | tf_op jit(solution)/shard_map/ppermute | solution.py:142
  8.4 4.8 %collective-permute-start.2 = (f32[2,56,128]{2,1,0:T(8,128)S(1)}, f32[2,56,128]{2,1,0:T(8,128)S(1)}, u32[]{:S(2)}, u32[]{:S(2)}) collective-permute-start(f32[2,56,128]{2,1,0:T(8,128)S(1)} %pad_maximum_fusion.4), channel_id=1, source_target_pairs={{0,9},{1,8},{2,11},{3,10},{4,13},{5,12},{6,15},{7,14},{8,1},{9,0},... | collective-permute-start | bytes 172040 | tf_op jit(solution)/shard_map/ppermute | solution.py:142
  12.7 5.0 %collective-permute-start.6 = (bf16[4,2,32,256]{3,2,1,0:T(8,128)(2,1)S(1)}, bf16[4,2,32,256]{3,2,1,0:T(8,128)(2,1)S(1)}, u32[]{:S(2)}, u32[]{:S(2)}) collective-permute-start(bf16[4,2,32,256]{3,2,1,0:T(8,128)(2,1)S(1)} %get-tuple-element.6), channel_id=1, source_target_pairs={{0,4},{1,5},{2,6},{3,7},{4,0},{5,1},{6,2},{7,3},{8,12},{9,13},{10,... | collective-permute-start | bytes 393224 | tf_op jit(solution)/shard_map/ppermute | solution.py:142
  13.2 5.5 %collective-permute-start.3 = (f32[4,56,128]{2,1,0:T(8,128)S(1)}, f32[4,56,128]{2,1,0:T(8,128)S(1)}, u32[]{:S(2)}, u32[]{:S(2)}) collective-permute-start(f32[4,56,128]{2,1,0:T(8,128)S(1)} %pad_maximum_fusion.3.refs_0_), channel_id=1, source_target_pairs={{0,2},{1,3},{2,0},{3,1},{4,6},{5,7},{6,4},{7,5},{8,10},{9,11},{10,... | collective-permute-start | bytes 344072 | tf_op jit(solution)/shard_map/ppermute | solution.py:142
  19.2 4.1 %collective-permute-start.7 = (f32[32,64]{1,0:T(8,128)S(1)}, f32[32,64]{1,0:T(8,128)S(1)}, u32[]{:S(2)}, u32[]{:S(2)}) collective-permute-start(f32[32,64]{1,0:T(8,128)S(1)} %score_other.3), channel_id=1, source_target_pairs={{0,9},{1,8},{2,11},{3,10},{4,13},{5,12},{6,15},{7,14},{8,1},{9,0},... | collective-permute-start | bytes 24584 | tf_op jit(solution)/shard_map/ppermute | solution.py:142
